TPU v7x, 256 devices: a whole 4x4x8 slice. The times are simulated.
256 devices in a mesh: row: 16 (over y_lo, x, core), col: 16 (over y_hi, z).
Axes of the slice: x: 4, y: 4 (y_hi: 2, y_lo: 2; y = y_hi * 2 + y_lo), z: 8, core: 2. Of those that a mesh axis runs over, the one named last changes fastest.
Arguments:
- amplitudes: bfloat16 [12288, 3072], P('row', 'col'), may hold values from -6 to 6
- integrals: bfloat16 [16, 192, 24576], P(None, 'row', 'col'), may hold values from -0.109375 to 0.109375
- residual_in: bfloat16 [12288, 24576], P('row', 'col'), may hold values from -3 to 3
- pair_class: int32 [128], P('row'), may hold values from 0 to 1
- cd_class: int32 [32], replicated, may hold values from 0 to 1
- ab_class: int32 [256], P('col'), may hold values from 0 to 1
Outputs:
- residual_out: bfloat16 [12288, 24576], P('row', 'col')
All inputs are finite; a program needn't handle non-finite values.
Results may differ from a plain program's by a relative error of at most 0.001.
Values may be sent and summed in bfloat16 or wider, within the bound.
No kernel may reach another device: no remote copies, remote signals or barrier semaphores. Data moves between devices by JAX's collectives and lax.ppermute only.
A program may use at most 128 MiB of HBM per device.

v0:
```python
import jax
import jax.numpy as jnp
from jax import lax
from jax.sharding import PartitionSpec as P

TILE = 96


def from_behind(value, axis, steps):
    count = lax.axis_size(axis)
    pairs = [(source, (source + steps) % count) for source in range(count)]
    return lax.ppermute(value, axis, pairs)


def local(amplitudes, integrals, residual_in, pair_class, cd_class, ab_class):
    pair_labels = jnp.repeat(pair_class, TILE)
    cd_labels = jnp.repeat(cd_class, TILE)
    ab_labels = jnp.repeat(ab_class, TILE)
    nothing = jnp.zeros((), jnp.bfloat16)
    slab_width = amplitudes.shape[1]

    def mask_amp(values, offset):
        labels = lax.dynamic_slice_in_dim(cd_labels, offset, values.shape[1])
        return jnp.where(pair_labels[:, None] == labels[None, :], values, nothing)

    def mask_int(values, offset):
        labels = lax.dynamic_slice_in_dim(cd_labels, offset, values.shape[0])
        return jnp.where(labels[:, None] == ab_labels[None, :], values, nothing)

    initial = residual_in.astype(jnp.float32)
    col_count = lax.axis_size("col")
    col_index = lax.axis_index("col")

    def contribute(ladder_sum, amp_slab, group_id):
        own_part = lax.dynamic_index_in_dim(integrals, group_id, 0, keepdims=False)
        int_panel = lax.all_gather(own_part, "row", axis=0, tiled=True)
        offset = group_id * slab_width
        return ladder_sum + jnp.dot(
            mask_amp(amp_slab, offset),
            mask_int(int_panel, offset),
            preferred_element_type=jnp.float32,
        )

    ladder_sum = contribute(initial, amplitudes, col_index)

    def advance(counter, state_pair):
        running, amp_slab = state_pair
        amp_slab = from_behind(amp_slab, "col", 1)
        group_id = (col_index - counter) % col_count
        return (contribute(running, amp_slab, group_id), amp_slab)

    ladder_sum, _ = lax.fori_loop(1, col_count, advance, (ladder_sum, amplitudes))
    return ladder_sum.astype(jnp.bfloat16)


def solution(mesh):
    return jax.shard_map(
        local,
        mesh=mesh,
        in_specs=(P("row", "col"), P(None, "row", "col"), P("row", "col"), P("row"), P(), P("col")),
        out_specs=P("row", "col"),
        check_vma=False,
    )
```

profile of v0, /device:TPU:12, one launch (start us, length us, event | category | flops | bytes accessed | tf_op | source)
XLA Modules:
  0.0 481.3 jit_solution(4971823204305039667)
XLA Ops:
  1.8 1.0 constant_dynamic-slice_fusion.1
  2.9 18.9 %all-gather.1 = bf16[1,192,1536]{2,0,1:T(2,128)(2,1)S(1)} all-gather(bf16[1,12,1536]{2,0,1:T(2,128)(2,1)S(1)} %constant_dynamic-slice_fusion.1), channel_id=3, replica_groups=mesh['row'=16,'col'=16] {'row'}, dimensions={1}, use_global_device_ids=true | all-gather | bytes 626688 | tf_op jit(solution)/shard_map/all_gather | solution.py:36
  23.4 4.8 convert_add_fusion
  28.2 449.2 %while.18 = (s32[]{:T(128)}, f32[768,1536]{1,0:T(8,128)}, bf16[768,192]{0,1:T(8,128)(2,1)S(1)}, s32[]{:T(128)}, s32[3072]{0:T(1024)S(1)}, /*index=5*/bf16[16,12,...) while((s32[]{:T(128)}, f32[768,1536]{1,0:T(8,128)}, ...), condition=%wide.region_1.2_spmd.clone, body=%wide.region_0.1_spmd.clone.sunk | while | flops 455049248 | bytes 12831454 | solution.py:52
  28.2 1.9 collective-permute-start
  31.5 22.8 %all-gather.4 = bf16[1,192,1536]{2,0,1:T(2,128)(2,1)S(1)} all-gather(bf16[1,12,1536]{2,0,1:T(2,128)(2,1)S(1)} %constant_dynamic-slice_fusion.3), channel_id=2, replica_groups=mesh['row'=16,'col'=16] {'row'}, dimensions={1}, use_global_device_ids=true | all-gather | bytes 626688 | tf_op jit(solution)/shard_map/while/body/eval_jaxpr/all_gather | solution.py:36
  54.3 5.4 %convolution_add_fusion.2 = f32[768,1536]{1,0:T(8,128)} fusion(f32[768,1536]{1,0:T(8,128)} %get-tuple-element.314, bf16[1,192,1536]{2,0,1:T(2,128)(2,1)S(1)} %all-gather.4, s32[1536]{0:T(1024)S(1)} %eq.206, s32[192]{0:T(256)S(1)} %dynamic_slice.38, bf16[768,192]{0,1:T(8,128)(2,1)S(1)} %collective-permute-done, s32[768]{0:T(1024)S(1)} %eq.207), kind=kOutput, calls=%fused_computation.2.clone.1 | convolution fusion | flops 455049216 | bytes 10331904 | tf_op jit(solution)/shard_map/while/body/eval_jaxpr/dot_general | solution.py:38
  59.8 1.0 constant_dynamic-slice_fusion.3
  61.2 23.0 %all-gather.4 = bf16[1,192,1536]{2,0,1:T(2,128)(2,1)S(1)} all-gather(bf16[1,12,1536]{2,0,1:T(2,128)(2,1)S(1)} %constant_dynamic-slice_fusion.3), channel_id=2, replica_groups=mesh['row'=16,'col'=16] {'row'}, dimensions={1}, use_global_device_ids=true | all-gather | bytes 626688 | tf_op jit(solution)/shard_map/while/body/eval_jaxpr/all_gather | solution.py:36
  84.2 5.4 %convolution_add_fusion.2 = f32[768,1536]{1,0:T(8,128)} fusion(f32[768,1536]{1,0:T(8,128)} %get-tuple-element.314, bf16[1,192,1536]{2,0,1:T(2,128)(2,1)S(1)} %all-gather.4, s32[1536]{0:T(1024)S(1)} %eq.206, s32[192]{0:T(256)S(1)} %dynamic_slice.38, bf16[768,192]{0,1:T(8,128)(2,1)S(1)} %collective-permute-done, s32[768]{0:T(1024)S(1)} %eq.207), kind=kOutput, calls=%fused_computation.2.clone.1 | convolution fusion | flops 455049216 | bytes 10331904 | tf_op jit(solution)/shard_map/while/body/eval_jaxpr/dot_general | solution.py:38
  89.6 1.0 constant_dynamic-slice_fusion.3
  91.0 23.0 %all-gather.4 = bf16[1,192,1536]{2,0,1:T(2,128)(2,1)S(1)} all-gather(bf16[1,12,1536]{2,0,1:T(2,128)(2,1)S(1)} %constant_dynamic-slice_fusion.3), channel_id=2, replica_groups=mesh['row'=16,'col'=16] {'row'}, dimensions={1}, use_global_device_ids=true | all-gather | bytes 626688 | tf_op jit(solution)/shard_map/while/body/eval_jaxpr/all_gather | solution.py:36
  114.0 5.4 %convolution_add_fusion.2 = f32[768,1536]{1,0:T(8,128)} fusion(f32[768,1536]{1,0:T(8,128)} %get-tuple-element.314, bf16[1,192,1536]{2,0,1:T(2,128)(2,1)S(1)} %all-gather.4, s32[1536]{0:T(1024)S(1)} %eq.206, s32[192]{0:T(256)S(1)} %dynamic_slice.38, bf16[768,192]{0,1:T(8,128)(2,1)S(1)} %collective-permute-done, s32[768]{0:T(1024)S(1)} %eq.207), kind=kOutput, calls=%fused_computation.2.clone.1 | convolution fusion | flops 455049216 | bytes 10331904 | tf_op jit(solution)/shard_map/while/body/eval_jaxpr/dot_general | solution.py:38
  119.4 1.0 constant_dynamic-slice_fusion.3
  120.8 23.0 %all-gather.4 = bf16[1,192,1536]{2,0,1:T(2,128)(2,1)S(1)} all-gather(bf16[1,12,1536]{2,0,1:T(2,128)(2,1)S(1)} %constant_dynamic-slice_fusion.3), channel_id=2, replica_groups=mesh['row'=16,'col'=16] {'row'}, dimensions={1}, use_global_device_ids=true | all-gather | bytes 626688 | tf_op jit(solution)/shard_map/while/body/eval_jaxpr/all_gather | solution.py:36
  143.8 5.4 %convolution_add_fusion.2 = f32[768,1536]{1,0:T(8,128)} fusion(f32[768,1536]{1,0:T(8,128)} %get-tuple-element.314, bf16[1,192,1536]{2,0,1:T(2,128)(2,1)S(1)} %all-gather.4, s32[1536]{0:T(1024)S(1)} %eq.206, s32[192]{0:T(256)S(1)} %dynamic_slice.38, bf16[768,192]{0,1:T(8,128)(2,1)S(1)} %collective-permute-done, s32[768]{0:T(1024)S(1)} %eq.207), kind=kOutput, calls=%fused_computation.2.clone.1 | convolution fusion | flops 455049216 | bytes 10331904 | tf_op jit(solution)/shard_map/while/body/eval_jaxpr/dot_general | solution.py:38
  149.2 1.0 constant_dynamic-slice_fusion.3
  150.7 23.0 %all-gather.4 = bf16[1,192,1536]{2,0,1:T(2,128)(2,1)S(1)} all-gather(bf16[1,12,1536]{2,0,1:T(2,128)(2,1)S(1)} %constant_dynamic-slice_fusion.3), channel_id=2, replica_groups=mesh['row'=16,'col'=16] {'row'}, dimensions={1}, use_global_device_ids=true | all-gather | bytes 626688 | tf_op jit(solution)/shard_map/while/body/eval_jaxpr/all_gather | solution.py:36
  173.7 5.4 %convolution_add_fusion.2 = f32[768,1536]{1,0:T(8,128)} fusion(f32[768,1536]{1,0:T(8,128)} %get-tuple-element.314, bf16[1,192,1536]{2,0,1:T(2,128)(2,1)S(1)} %all-gather.4, s32[1536]{0:T(1024)S(1)} %eq.206, s32[192]{0:T(256)S(1)} %dynamic_slice.38, bf16[768,192]{0,1:T(8,128)(2,1)S(1)} %collective-permute-done, s32[768]{0:T(1024)S(1)} %eq.207), kind=kOutput, calls=%fused_computation.2.clone.1 | convolution fusion | flops 455049216 | bytes 10331904 | tf_op jit(solution)/shard_map/while/body/eval_jaxpr/dot_general | solution.py:38
  179.1 1.0 constant_dynamic-slice_fusion.3
  180.5 23.0 %all-gather.4 = bf16[1,192,1536]{2,0,1:T(2,128)(2,1)S(1)} all-gather(bf16[1,12,1536]{2,0,1:T(2,128)(2,1)S(1)} %constant_dynamic-slice_fusion.3), channel_id=2, replica_groups=mesh['row'=16,'col'=16] {'row'}, dimensions={1}, use_global_device_ids=true | all-gather | bytes 626688 | tf_op jit(solution)/shard_map/while/body/eval_jaxpr/all_gather | solution.py:36
  203.5 5.4 %convolution_add_fusion.2 = f32[768,1536]{1,0:T(8,128)} fusion(f32[768,1536]{1,0:T(8,128)} %get-tuple-element.314, bf16[1,192,1536]{2,0,1:T(2,128)(2,1)S(1)} %all-gather.4, s32[1536]{0:T(1024)S(1)} %eq.206, s32[192]{0:T(256)S(1)} %dynamic_slice.38, bf16[768,192]{0,1:T(8,128)(2,1)S(1)} %collective-permute-done, s32[768]{0:T(1024)S(1)} %eq.207), kind=kOutput, calls=%fused_computation.2.clone.1 | convolution fusion | flops 455049216 | bytes 10331904 | tf_op jit(solution)/shard_map/while/body/eval_jaxpr/dot_general | solution.py:38
  208.9 1.0 constant_dynamic-slice_fusion.3
  210.3 23.0 %all-gather.4 = bf16[1,192,1536]{2,0,1:T(2,128)(2,1)S(1)} all-gather(bf16[1,12,1536]{2,0,1:T(2,128)(2,1)S(1)} %constant_dynamic-slice_fusion.3), channel_id=2, replica_groups=mesh['row'=16,'col'=16] {'row'}, dimensions={1}, use_global_device_ids=true | all-gather | bytes 626688 | tf_op jit(solution)/shard_map/while/body/eval_jaxpr/all_gather | solution.py:36
  233.3 5.4 %convolution_add_fusion.2 = f32[768,1536]{1,0:T(8,128)} fusion(f32[768,1536]{1,0:T(8,128)} %get-tuple-element.314, bf16[1,192,1536]{2,0,1:T(2,128)(2,1)S(1)} %all-gather.4, s32[1536]{0:T(1024)S(1)} %eq.206, s32[192]{0:T(256)S(1)} %dynamic_slice.38, bf16[768,192]{0,1:T(8,128)(2,1)S(1)} %collective-permute-done, s32[768]{0:T(1024)S(1)} %eq.207), kind=kOutput, calls=%fused_computation.2.clone.1 | convolution fusion | flops 455049216 | bytes 10331904 | tf_op jit(solution)/shard_map/while/body/eval_jaxpr/dot_general | solution.py:38
  238.7 1.0 constant_dynamic-slice_fusion.3
  240.1 23.0 %all-gather.4 = bf16[1,192,1536]{2,0,1:T(2,128)(2,1)S(1)} all-gather(bf16[1,12,1536]{2,0,1:T(2,128)(2,1)S(1)} %constant_dynamic-slice_fusion.3), channel_id=2, replica_groups=mesh['row'=16,'col'=16] {'row'}, dimensions={1}, use_global_device_ids=true | all-gather | bytes 626688 | tf_op jit(solution)/shard_map/while/body/eval_jaxpr/all_gather | solution.py:36
  263.1 5.4 %convolution_add_fusion.2 = f32[768,1536]{1,0:T(8,128)} fusion(f32[768,1536]{1,0:T(8,128)} %get-tuple-element.314, bf16[1,192,1536]{2,0,1:T(2,128)(2,1)S(1)} %all-gather.4, s32[1536]{0:T(1024)S(1)} %eq.206, s32[192]{0:T(256)S(1)} %dynamic_slice.38, bf16[768,192]{0,1:T(8,128)(2,1)S(1)} %collective-permute-done, s32[768]{0:T(1024)S(1)} %eq.207), kind=kOutput, calls=%fused_computation.2.clone.1 | convolution fusion | flops 455049216 | bytes 10331904 | tf_op jit(solution)/shard_map/while/body/eval_jaxpr/dot_general | solution.py:38
  268.6 1.0 constant_dynamic-slice_fusion.3
  270.0 23.0 %all-gather.4 = bf16[1,192,1536]{2,0,1:T(2,128)(2,1)S(1)} all-gather(bf16[1,12,1536]{2,0,1:T(2,128)(2,1)S(1)} %constant_dynamic-slice_fusion.3), channel_id=2, replica_groups=mesh['row'=16,'col'=16] {'row'}, dimensions={1}, use_global_device_ids=true | all-gather | bytes 626688 | tf_op jit(solution)/shard_map/while/body/eval_jaxpr/all_gather | solution.py:36
  293.0 5.4 %convolution_add_fusion.2 = f32[768,1536]{1,0:T(8,128)} fusion(f32[768,1536]{1,0:T(8,128)} %get-tuple-element.314, bf16[1,192,1536]{2,0,1:T(2,128)(2,1)S(1)} %all-gather.4, s32[1536]{0:T(1024)S(1)} %eq.206, s32[192]{0:T(256)S(1)} %dynamic_slice.38, bf16[768,192]{0,1:T(8,128)(2,1)S(1)} %collective-permute-done, s32[768]{0:T(1024)S(1)} %eq.207), kind=kOutput, calls=%fused_computation.2.clone.1 | convolution fusion | flops 455049216 | bytes 10331904 | tf_op jit(solution)/shard_map/while/body/eval_jaxpr/dot_general | solution.py:38
  298.4 1.0 constant_dynamic-slice_fusion.3
  299.8 23.0 %all-gather.4 = bf16[1,192,1536]{2,0,1:T(2,128)(2,1)S(1)} all-gather(bf16[1,12,1536]{2,0,1:T(2,128)(2,1)S(1)} %constant_dynamic-slice_fusion.3), channel_id=2, replica_groups=mesh['row'=16,'col'=16] {'row'}, dimensions={1}, use_global_device_ids=true | all-gather | bytes 626688 | tf_op jit(solution)/shard_map/while/body/eval_jaxpr/all_gather | solution.py:36
  322.8 5.4 %convolution_add_fusion.2 = f32[768,1536]{1,0:T(8,128)} fusion(f32[768,1536]{1,0:T(8,128)} %get-tuple-element.314, bf16[1,192,1536]{2,0,1:T(2,128)(2,1)S(1)} %all-gather.4, s32[1536]{0:T(1024)S(1)} %eq.206, s32[192]{0:T(256)S(1)} %dynamic_slice.38, bf16[768,192]{0,1:T(8,128)(2,1)S(1)} %collective-permute-done, s32[768]{0:T(1024)S(1)} %eq.207), kind=kOutput, calls=%fused_computation.2.clone.1 | convolution fusion | flops 455049216 | bytes 10331904 | tf_op jit(solution)/shard_map/while/body/eval_jaxpr/dot_general | solution.py:38
  328.2 1.0 constant_dynamic-slice_fusion.3
  329.6 23.0 %all-gather.4 = bf16[1,192,1536]{2,0,1:T(2,128)(2,1)S(1)} all-gather(bf16[1,12,1536]{2,0,1:T(2,128)(2,1)S(1)} %constant_dynamic-slice_fusion.3), channel_id=2, replica_groups=mesh['row'=16,'col'=16] {'row'}, dimensions={1}, use_global_device_ids=true | all-gather | bytes 626688 | tf_op jit(solution)/shard_map/while/body/eval_jaxpr/all_gather | solution.py:36
  352.6 5.4 %convolution_add_fusion.2 = f32[768,1536]{1,0:T(8,128)} fusion(f32[768,1536]{1,0:T(8,128)} %get-tuple-element.314, bf16[1,192,1536]{2,0,1:T(2,128)(2,1)S(1)} %all-gather.4, s32[1536]{0:T(1024)S(1)} %eq.206, s32[192]{0:T(256)S(1)} %dynamic_slice.38, bf16[768,192]{0,1:T(8,128)(2,1)S(1)} %collective-permute-done, s32[768]{0:T(1024)S(1)} %eq.207), kind=kOutput, calls=%fused_computation.2.clone.1 | convolution fusion | flops 455049216 | bytes 10331904 | tf_op jit(solution)/shard_map/while/body/eval_jaxpr/dot_general | solution.py:38
  358.0 1.0 constant_dynamic-slice_fusion.3
  359.4 23.0 %all-gather.4 = bf16[1,192,1536]{2,0,1:T(2,128)(2,1)S(1)} all-gather(bf16[1,12,1536]{2,0,1:T(2,128)(2,1)S(1)} %constant_dynamic-slice_fusion.3), channel_id=2, replica_groups=mesh['row'=16,'col'=16] {'row'}, dimensions={1}, use_global_device_ids=true | all-gather | bytes 626688 | tf_op jit(solution)/shard_map/while/body/eval_jaxpr/all_gather | solution.py:36
  382.4 5.4 %convolution_add_fusion.2 = f32[768,1536]{1,0:T(8,128)} fusion(f32[768,1536]{1,0:T(8,128)} %get-tuple-element.314, bf16[1,192,1536]{2,0,1:T(2,128)(2,1)S(1)} %all-gather.4, s32[1536]{0:T(1024)S(1)} %eq.206, s32[192]{0:T(256)S(1)} %dynamic_slice.38, bf16[768,192]{0,1:T(8,128)(2,1)S(1)} %collective-permute-done, s32[768]{0:T(1024)S(1)} %eq.207), kind=kOutput, calls=%fused_computation.2.clone.1 | convolution fusion | flops 455049216 | bytes 10331904 | tf_op jit(solution)/shard_map/while/body/eval_jaxpr/dot_general | solution.py:38
  387.8 1.0 constant_dynamic-slice_fusion.3
  389.3 23.0 %all-gather.4 = bf16[1,192,1536]{2,0,1:T(2,128)(2,1)S(1)} all-gather(bf16[1,12,1536]{2,0,1:T(2,128)(2,1)S(1)} %constant_dynamic-slice_fusion.3), channel_id=2, replica_groups=mesh['row'=16,'col'=16] {'row'}, dimensions={1}, use_global_device_ids=true | all-gather | bytes 626688 | tf_op jit(solution)/shard_map/while/body/eval_jaxpr/all_gather | solution.py:36
  412.3 5.4 %convolution_add_fusion.2 = f32[768,1536]{1,0:T(8,128)} fusion(f32[768,1536]{1,0:T(8,128)} %get-tuple-element.314, bf16[1,192,1536]{2,0,1:T(2,128)(2,1)S(1)} %all-gather.4, s32[1536]{0:T(1024)S(1)} %eq.206, s32[192]{0:T(256)S(1)} %dynamic_slice.38, bf16[768,192]{0,1:T(8,128)(2,1)S(1)} %collective-permute-done, s32[768]{0:T(1024)S(1)} %eq.207), kind=kOutput, calls=%fused_computation.2.clone.1 | convolution fusion | flops 455049216 | bytes 10331904 | tf_op jit(solution)/shard_map/while/body/eval_jaxpr/dot_general | solution.py:38
  419.1 23.0 %all-gather.4 = bf16[1,192,1536]{2,0,1:T(2,128)(2,1)S(1)} all-gather(bf16[1,12,1536]{2,0,1:T(2,128)(2,1)S(1)} %constant_dynamic-slice_fusion.3), channel_id=2, replica_groups=mesh['row'=16,'col'=16] {'row'}, dimensions={1}, use_global_device_ids=true | all-gather | bytes 626688 | tf_op jit(solution)/shard_map/while/body/eval_jaxpr/all_gather | solution.py:36
  442.1 5.4 %convolution_add_fusion.2 = f32[768,1536]{1,0:T(8,128)} fusion(f32[768,1536]{1,0:T(8,128)} %get-tuple-element.314, bf16[1,192,1536]{2,0,1:T(2,128)(2,1)S(1)} %all-gather.4, s32[1536]{0:T(1024)S(1)} %eq.206, s32[192]{0:T(256)S(1)} %dynamic_slice.38, bf16[768,192]{0,1:T(8,128)(2,1)S(1)} %collective-permute-done, s32[768]{0:T(1024)S(1)} %eq.207), kind=kOutput, calls=%fused_computation.2.clone.1 | convolution fusion | flops 455049216 | bytes 10331904 | tf_op jit(solution)/shard_map/while/body/eval_jaxpr/dot_general | solution.py:38
  448.9 23.0 %all-gather.4 = bf16[1,192,1536]{2,0,1:T(2,128)(2,1)S(1)} all-gather(bf16[1,12,1536]{2,0,1:T(2,128)(2,1)S(1)} %constant_dynamic-slice_fusion.3), channel_id=2, replica_groups=mesh['row'=16,'col'=16] {'row'}, dimensions={1}, use_global_device_ids=true | all-gather | bytes 626688 | tf_op jit(solution)/shard_map/while/body/eval_jaxpr/all_gather | solution.py:36
  471.9 5.4 %convolution_add_fusion.2 = f32[768,1536]{1,0:T(8,128)} fusion(f32[768,1536]{1,0:T(8,128)} %get-tuple-element.314, bf16[1,192,1536]{2,0,1:T(2,128)(2,1)S(1)} %all-gather.4, s32[1536]{0:T(1024)S(1)} %eq.206, s32[192]{0:T(256)S(1)} %dynamic_slice.38, bf16[768,192]{0,1:T(8,128)(2,1)S(1)} %collective-permute-done, s32[768]{0:T(1024)S(1)} %eq.207), kind=kOutput, calls=%fused_computation.2.clone.1 | convolution fusion | flops 455049216 | bytes 10331904 | tf_op jit(solution)/shard_map/while/body/eval_jaxpr/dot_general | solution.py:38
  477.3 4.0 convert_element_type.7
  (134 shorter events, 12.4 us)
Async XLA Ops:
  23.4 4.8 copy-start
  23.4 4.8 copy-start.1
  28.2 26.2 %collective-permute-start = (bf16[768,192]{0,1:T(8,128)(2,1)S(1)}, bf16[768,192]{0,1:T(8,128)(2,1)S(1)}, u32[]{:S(2)}, u32[]{:S(2)}) collective-permute-start(bf16[768,192]{0,1:T(8,128)(2,1)S(1)} %get-tuple-element.315), channel_id=1, source_target_pairs={{0,1},{1,2},{2,3},{3,4},{4,5},{5,6},{6,7},{7,8},{8,9},{9,10},{10,1... | collective-permute-start | bytes 884744 | tf_op jit(solution)/shard_map/while/body/eval_jaxpr/ppermute | solution.py:12
  59.8 24.4 %collective-permute-start = (bf16[768,192]{0,1:T(8,128)(2,1)S(1)}, bf16[768,192]{0,1:T(8,128)(2,1)S(1)}, u32[]{:S(2)}, u32[]{:S(2)}) collective-permute-start(bf16[768,192]{0,1:T(8,128)(2,1)S(1)} %get-tuple-element.315), channel_id=1, source_target_pairs={{0,1},{1,2},{2,3},{3,4},{4,5},{5,6},{6,7},{7,8},{8,9},{9,10},{10,1... | collective-permute-start | bytes 884744 | tf_op jit(solution)/shard_map/while/body/eval_jaxpr/ppermute | solution.py:12
  89.6 24.4 %collective-permute-start = (bf16[768,192]{0,1:T(8,128)(2,1)S(1)}, bf16[768,192]{0,1:T(8,128)(2,1)S(1)}, u32[]{:S(2)}, u32[]{:S(2)}) collective-permute-start(bf16[768,192]{0,1:T(8,128)(2,1)S(1)} %get-tuple-element.315), channel_id=1, source_target_pairs={{0,1},{1,2},{2,3},{3,4},{4,5},{5,6},{6,7},{7,8},{8,9},{9,10},{10,1... | collective-permute-start | bytes 884744 | tf_op jit(solution)/shard_map/while/body/eval_jaxpr/ppermute | solution.py:12
  119.4 24.4 %collective-permute-start = (bf16[768,192]{0,1:T(8,128)(2,1)S(1)}, bf16[768,192]{0,1:T(8,128)(2,1)S(1)}, u32[]{:S(2)}, u32[]{:S(2)}) collective-permute-start(bf16[768,192]{0,1:T(8,128)(2,1)S(1)} %get-tuple-element.315), channel_id=1, source_target_pairs={{0,1},{1,2},{2,3},{3,4},{4,5},{5,6},{6,7},{7,8},{8,9},{9,10},{10,1... | collective-permute-start | bytes 884744 | tf_op jit(solution)/shard_map/while/body/eval_jaxpr/ppermute | solution.py:12
  149.2 24.4 %collective-permute-start = (bf16[768,192]{0,1:T(8,128)(2,1)S(1)}, bf16[768,192]{0,1:T(8,128)(2,1)S(1)}, u32[]{:S(2)}, u32[]{:S(2)}) collective-permute-start(bf16[768,192]{0,1:T(8,128)(2,1)S(1)} %get-tuple-element.315), channel_id=1, source_target_pairs={{0,1},{1,2},{2,3},{3,4},{4,5},{5,6},{6,7},{7,8},{8,9},{9,10},{10,1... | collective-permute-start | bytes 884744 | tf_op jit(solution)/shard_map/while/body/eval_jaxpr/ppermute | solution.py:12
  179.1 24.4 %collective-permute-start = (bf16[768,192]{0,1:T(8,128)(2,1)S(1)}, bf16[768,192]{0,1:T(8,128)(2,1)S(1)}, u32[]{:S(2)}, u32[]{:S(2)}) collective-permute-start(bf16[768,192]{0,1:T(8,128)(2,1)S(1)} %get-tuple-element.315), channel_id=1, source_target_pairs={{0,1},{1,2},{2,3},{3,4},{4,5},{5,6},{6,7},{7,8},{8,9},{9,10},{10,1... | collective-permute-start | bytes 884744 | tf_op jit(solution)/shard_map/while/body/eval_jaxpr/ppermute | solution.py:12
  208.9 24.4 %collective-permute-start = (bf16[768,192]{0,1:T(8,128)(2,1)S(1)}, bf16[768,192]{0,1:T(8,128)(2,1)S(1)}, u32[]{:S(2)}, u32[]{:S(2)}) collective-permute-start(bf16[768,192]{0,1:T(8,128)(2,1)S(1)} %get-tuple-element.315), channel_id=1, source_target_pairs={{0,1},{1,2},{2,3},{3,4},{4,5},{5,6},{6,7},{7,8},{8,9},{9,10},{10,1... | collective-permute-start | bytes 884744 | tf_op jit(solution)/shard_map/while/body/eval_jaxpr/ppermute | solution.py:12
  238.7 24.4 %collective-permute-start = (bf16[768,192]{0,1:T(8,128)(2,1)S(1)}, bf16[768,192]{0,1:T(8,128)(2,1)S(1)}, u32[]{:S(2)}, u32[]{:S(2)}) collective-permute-start(bf16[768,192]{0,1:T(8,128)(2,1)S(1)} %get-tuple-element.315), channel_id=1, source_target_pairs={{0,1},{1,2},{2,3},{3,4},{4,5},{5,6},{6,7},{7,8},{8,9},{9,10},{10,1... | collective-permute-start | bytes 884744 | tf_op jit(solution)/shard_map/while/body/eval_jaxpr/ppermute | solution.py:12
  268.5 24.4 %collective-permute-start = (bf16[768,192]{0,1:T(8,128)(2,1)S(1)}, bf16[768,192]{0,1:T(8,128)(2,1)S(1)}, u32[]{:S(2)}, u32[]{:S(2)}) collective-permute-start(bf16[768,192]{0,1:T(8,128)(2,1)S(1)} %get-tuple-element.315), channel_id=1, source_target_pairs={{0,1},{1,2},{2,3},{3,4},{4,5},{5,6},{6,7},{7,8},{8,9},{9,10},{10,1... | collective-permute-start | bytes 884744 | tf_op jit(solution)/shard_map/while/body/eval_jaxpr/ppermute | solution.py:12
  298.4 24.4 %collective-permute-start = (bf16[768,192]{0,1:T(8,128)(2,1)S(1)}, bf16[768,192]{0,1:T(8,128)(2,1)S(1)}, u32[]{:S(2)}, u32[]{:S(2)}) collective-permute-start(bf16[768,192]{0,1:T(8,128)(2,1)S(1)} %get-tuple-element.315), channel_id=1, source_target_pairs={{0,1},{1,2},{2,3},{3,4},{4,5},{5,6},{6,7},{7,8},{8,9},{9,10},{10,1... | collective-permute-start | bytes 884744 | tf_op jit(solution)/shard_map/while/body/eval_jaxpr/ppermute | solution.py:12
  328.2 24.4 %collective-permute-start = (bf16[768,192]{0,1:T(8,128)(2,1)S(1)}, bf16[768,192]{0,1:T(8,128)(2,1)S(1)}, u32[]{:S(2)}, u32[]{:S(2)}) collective-permute-start(bf16[768,192]{0,1:T(8,128)(2,1)S(1)} %get-tuple-element.315), channel_id=1, source_target_pairs={{0,1},{1,2},{2,3},{3,4},{4,5},{5,6},{6,7},{7,8},{8,9},{9,10},{10,1... | collective-permute-start | bytes 884744 | tf_op jit(solution)/shard_map/while/body/eval_jaxpr/ppermute | solution.py:12
  358.0 24.4 %collective-permute-start = (bf16[768,192]{0,1:T(8,128)(2,1)S(1)}, bf16[768,192]{0,1:T(8,128)(2,1)S(1)}, u32[]{:S(2)}, u32[]{:S(2)}) collective-permute-start(bf16[768,192]{0,1:T(8,128)(2,1)S(1)} %get-tuple-element.315), channel_id=1, source_target_pairs={{0,1},{1,2},{2,3},{3,4},{4,5},{5,6},{6,7},{7,8},{8,9},{9,10},{10,1... | collective-permute-start | bytes 884744 | tf_op jit(solution)/shard_map/while/body/eval_jaxpr/ppermute | solution.py:12
  387.8 24.4 %collective-permute-start = (bf16[768,192]{0,1:T(8,128)(2,1)S(1)}, bf16[768,192]{0,1:T(8,128)(2,1)S(1)}, u32[]{:S(2)}, u32[]{:S(2)}) collective-permute-start(bf16[768,192]{0,1:T(8,128)(2,1)S(1)} %get-tuple-element.315), channel_id=1, source_target_pairs={{0,1},{1,2},{2,3},{3,4},{4,5},{5,6},{6,7},{7,8},{8,9},{9,10},{10,1... | collective-permute-start | bytes 884744 | tf_op jit(solution)/shard_map/while/body/eval_jaxpr/ppermute | solution.py:12
  417.7 24.4 %collective-permute-start = (bf16[768,192]{0,1:T(8,128)(2,1)S(1)}, bf16[768,192]{0,1:T(8,128)(2,1)S(1)}, u32[]{:S(2)}, u32[]{:S(2)}) collective-permute-start(bf16[768,192]{0,1:T(8,128)(2,1)S(1)} %get-tuple-element.315), channel_id=1, source_target_pairs={{0,1},{1,2},{2,3},{3,4},{4,5},{5,6},{6,7},{7,8},{8,9},{9,10},{10,1... | collective-permute-start | bytes 884744 | tf_op jit(solution)/shard_map/while/body/eval_jaxpr/ppermute | solution.py:12
  447.5 24.4 %collective-permute-start = (bf16[768,192]{0,1:T(8,128)(2,1)S(1)}, bf16[768,192]{0,1:T(8,128)(2,1)S(1)}, u32[]{:S(2)}, u32[]{:S(2)}) collective-permute-start(bf16[768,192]{0,1:T(8,128)(2,1)S(1)} %get-tuple-element.315), channel_id=1, source_target_pairs={{0,1},{1,2},{2,3},{3,4},{4,5},{5,6},{6,7},{7,8},{8,9},{9,10},{10,1... | collective-permute-start | bytes 884744 | tf_op jit(solution)/shard_map/while/body/eval_jaxpr/ppermute | solution.py:12
where the time goes:
time: 488 us; the launch traced here: 481 us
  blocking collectives  363 us (74%)
  matrix products  85.9 us (18%)
  local copies, waits for them, and re-layouts  25.9 us (5%)
    all_gather x16, blocking collectives, contribute(): int_panel = lax.all_gather(own_part, 'row', axis=0, tiled=True)  363 us
    dot_general x16, matrix products, contribute(): jnp.dot(mask_amp(amp_slab, offset), mask_int(int_panel, offset), preferre...  85.9 us
    dynamic_slice x16, local copies, waits for them, and re-layouts, contribute(): own_part = lax.dynamic_index_in_dim(integrals, group_id, 0, keepdims=False)  16.6 us
  transfers between devices with their start and end apart: 15, of which 0 were waited for; matrix products, arithmetic and copies ran while one was open for 4% of the time, Pallas kernels for 0%

commit v1 on v0

v1 whole, which is shorter than its diff:
```python
import jax
import jax.numpy as jnp
import numpy as np
from jax import lax
from jax.sharding import Mesh, PartitionSpec as P

TILE = 96
FINE = ("ylo", "x", "core", "yhi", "z")
ROW = ("ylo", "x", "core")
COL = ("yhi", "z")


def shift(value, axis, steps):
    count = lax.axis_size(axis)
    return lax.ppermute(value, axis, [(i, (i + steps) % count) for i in range(count)])


def gather_amp(own):
    deep, wide = own.shape
    half = deep // 2
    count = lax.axis_size("z")
    z, side = lax.axis_index("z"), lax.axis_index("yhi")
    other = shift(own, "yhi", 1)
    found = []
    for chunk, plane in ((own, side), (other, 1 - side)):
        found.append((chunk, plane, z, 0))
        up = down = chunk
        for step in range(1, count // 2):
            up, down = shift(up, "z", 1), shift(down, "z", -1)
            found.append((up, plane, (z - step) % count, 0))
            found.append((down, plane, (z + step) % count, 0))
        far = (z + count // 2) % count
        found.append((shift(up[:half], "z", 1), plane, far, 0))
        found.append((shift(down[half:], "z", -1), plane, far, half))
    whole = jnp.zeros((2 * count, deep, wide), own.dtype)
    for chunk, plane, place, row in found:
        whole = lax.dynamic_update_slice(whole, chunk[None], (plane * count + place, row, 0))
    return whole


def local(amplitudes, integrals, residual_in, pair_class, cd_class, ab_class):
    groups, part, width = integrals.shape
    rows = 16
    deep = amplitudes.shape[1]
    pair_labels = jnp.repeat(pair_class, TILE)
    ab_labels = jnp.repeat(ab_class, TILE)
    group = lax.axis_index("yhi") * 8 + lax.axis_index("z")
    own_labels = lax.dynamic_slice_in_dim(jnp.repeat(cd_class, TILE), group * deep, deep)

    panel = lax.all_gather(integrals.reshape(groups * part, width), ROW, axis=0, tiled=True)

    own = jnp.where(own_labels[:, None] == pair_labels[None, :], amplitudes.T, 0)
    whole = gather_amp(own.astype(jnp.bfloat16))
    amp = whole.reshape(groups, rows, part, -1).transpose(1, 0, 2, 3).reshape(groups * deep, -1)

    ladder = lax.dot_general(amp, panel, (((0,), (0,)), ((), ())), preferred_element_type=jnp.float32)
    ladder = jnp.where(pair_labels[:, None] == ab_labels[None, :], ladder, 0.0)
    return (residual_in.astype(jnp.float32) + ladder).astype(jnp.bfloat16)


def solution(mesh):
    fine = Mesh(mesh.devices.reshape(2, 4, 2, 2, 8), FINE)
    return jax.shard_map(
        local,
        mesh=fine,
        in_specs=(P(ROW, COL), P(None, ROW, COL), P(ROW, COL), P(ROW), P(), P(COL)),
        out_specs=P(ROW, COL),
        check_vma=False,
    )
```

time: 488 us -> 317 us (0.65)
  blocking collectives: 363 us -> 0 us
  local copies, waits for them, and re-layouts: 25.9 us -> 233 us
  matrix products: 85.9 us -> 12.8 us
  starting transfers between devices: 1.96 us -> 33.6 us
  waiting for transfers between devices: 0.04 us -> 17.4 us
  between operations: 0.01 us -> 13.6 us
    all_gather x16 -> x0, blocking collectives: 363 us -> none  [contribute(): int_panel = lax.all_gather(own_part, 'row', axis=0, tiled=True)]
    dynamic_update_slice x0 -> x18, local copies, waits for them, and re-layouts: none -> 190 us  [gather_amp(): lax.dynamic_update_slice(whole, chunk[None], (plane * count + place, row,...]
    dot_general x16 -> x1, matrix products: 85.9 us -> 12.8 us  [local(): lax.dot_general(amp, panel, (((0,), (0,)), ((), ())), preferred_element_t...]
    ppermute x15 -> x17, starting transfers between devices: 1.96 us -> 33.6 us  [shift(): lax.ppermute(value, axis, [(i, (i + steps) % count) for i in range(count)])]
    broadcast_in_dim x1 -> x20, local copies, waits for them, and re-layouts: 0.72 us -> 20.6 us  [the longest x18 17.5 us: gather_amp(): chunk[None]]
    dynamic_slice x32 -> x1, local copies, waits for them, and re-layouts: 17.9 us -> 0.08 us  [local(): lax.dynamic_slice_in_dim(jnp.repeat(cd_class, TILE), group * deep, deep)]
    ppermute x15 -> x17, waiting for transfers between devices: 0.04 us -> 17.4 us  [shift(): lax.ppermute(value, axis, [(i, (i + steps) % count) for i in range(count)])]
    reshape x1 -> x3, local copies, waits for them, and re-layouts: 0.07 us -> 9.55 us  [the longest x1 8.54 us: local(): whole.reshape(groups, rows, part, -1).transpose(1, 0, 2, 3)]
  transfers between devices with their start and end apart: 15 -> 18, of which waited for: 0 -> 6; matrix products, arithmetic and copies ran while one was open for 4% -> 74% of each run, Pallas kernels for 0% -> 0%
where the time goes in v1:
time: 317 us; the launch traced here: 312 us
  local copies, waits for them, and re-layouts  233 us (74%)
  starting transfers between devices  33.6 us (11%)
  waiting for transfers between devices  17.4 us (5%)
  between operations  13.6 us (4%)
  matrix products  12.8 us (4%)
    dynamic_update_slice x18, local copies, waits for them, and re-layouts, gather_amp(): lax.dynamic_update_slice(whole, chunk[None], (plane * count + place, row,...  190 us
    ppermute x17, starting transfers between devices, shift(): lax.ppermute(value, axis, [(i, (i + steps) % count) for i in range(count)])  33.6 us
    broadcast_in_dim x18, local copies, waits for them, and re-layouts, gather_amp(): chunk[None]  17.5 us
    ppermute x17, waiting for transfers between devices, shift(): lax.ppermute(value, axis, [(i, (i + steps) % count) for i in range(count)])  17.4 us
    dot_general x1, matrix products, local(): lax.dot_general(amp, panel, (((0,), (0,)), ((), ())), preferred_element_t...  12.8 us
    reshape x1, local copies, waits for them, and re-layouts, local(): whole.reshape(groups, rows, part, -1).transpose(1, 0, 2, 3)  8.54 us
    transpose x1, local copies, waits for them, and re-layouts, local(): whole.reshape(groups, rows, part, -1).transpose(1, 0, 2, 3)  7.15 us
  transfers between devices with their start and end apart: 18, of which 6 were waited for; matrix products, arithmetic and copies ran while one was open for 74% of the time, Pallas kernels for 0%

profile of v1, /device:TPU:12, one launch (start us, length us, event | category | flops | bytes accessed | tf_op | source)
XLA Modules:
  0.0 311.6 jit_solution(14068679249403768013)
XLA Ops:
  6.5 1.4 copy.45
  11.7 2.4 collective-permute-start.8
  14.1 1.9 collective-permute-start
  16.0 3.9 %collective-permute-start.1 = (bf16[192,768]{1,0:T(8,128)(2,1)S(1)}, bf16[192,768]{1,0:T(8,128)(2,1)S(1)}, u32[]{:S(2)}, u32[]{:S(2)}) collective-permute-start(bf16[192,768]{1,0:T(8,128)(2,1)S(1)} %compare_select_fusion), channel_id=1, source_target_pairs={{0,7},{1,0},{2,1},{3,2},{4,3},{5,4},{6,5},{7,6},{8,15},{9,8},{10,9... | collective-permute-start | bytes 884744 | tf_op jit(solution)/shard_map/ppermute | solution.py:15
  20.0 2.1 collective-permute-done.8
  22.1 1.9 collective-permute-start.9
  24.0 3.9 %collective-permute-start.10 = (bf16[192,768]{1,0:T(8,128)(2,1)S(1)}, bf16[192,768]{1,0:T(8,128)(2,1)S(1)}, u32[]{:S(2)}, u32[]{:S(2)}) collective-permute-start(bf16[192,768]{1,0:T(8,128)(2,1)S(1)} %collective-permute-done.8), channel_id=1, source_target_pairs={{0,7},{1,0},{2,1},{3,2},{4,3},{5,4},{6,5},{7,6},{8,15},{9,8},{10,9... | collective-permute-start | bytes 884744 | tf_op jit(solution)/shard_map/ppermute | solution.py:15
  28.0 3.2 %collective-permute-start.3 = (bf16[192,768]{1,0:T(8,128)(2,1)S(1)}, bf16[192,768]{1,0:T(8,128)(2,1)}, u32[]{:S(2)}, u32[]{:S(2)}) collective-permute-start(bf16[192,768]{1,0:T(8,128)(2,1)S(1)} %collective-permute-done.1), channel_id=1, source_target_pairs={{0,7},{1,0},{2,1},{3,2},{4,3},{5,4},{6,5},{7,6},{8,15},{9,8},{10,9... | collective-permute-start | bytes 884744 | tf_op jit(solution)/shard_map/ppermute | solution.py:15
  31.2 4.7 %collective-permute-done.9 = bf16[192,768]{1,0:T(8,128)(2,1)S(1)} collective-permute-done((bf16[192,768]{1,0:T(8,128)(2,1)S(1)}, bf16[192,768]{1,0:T(8,128)(2,1)S(1)}, u32[]{:S(2)}, u32[]{:S(2)}) %collective-permute-start.9) | collective-permute-done | bytes 294944 | tf_op jit(solution)/shard_map/ppermute | solution.py:15
  35.9 3.2 %collective-permute-start.12 = (bf16[192,768]{1,0:T(8,128)(2,1)S(1)}, bf16[192,768]{1,0:T(8,128)(2,1)}, u32[]{:S(2)}, u32[]{:S(2)}) collective-permute-start(bf16[192,768]{1,0:T(8,128)(2,1)S(1)} %collective-permute-done.10), channel_id=1, source_target_pairs={{0,7},{1,0},{2,1},{3,2},{4,3},{5,4},{6,5},{7,6},{8,15},{9,8},{10,9... | collective-permute-start | bytes 884744 | tf_op jit(solution)/shard_map/ppermute | solution.py:15
  39.1 3.2 %collective-permute-done.2 = bf16[192,768]{1,0:T(8,128)(2,1)} collective-permute-done((bf16[192,768]{1,0:T(8,128)(2,1)S(1)}, bf16[192,768]{1,0:T(8,128)(2,1)}, u32[]{:S(2)}, u32[]{:S(2)}) %collective-permute-start.2) | collective-permute-done | bytes 294944 | tf_op jit(solution)/shard_map/ppermute | solution.py:15
  42.3 3.2 %collective-permute-start.5 = (bf16[192,768]{1,0:T(8,128)(2,1)}, bf16[192,768]{1,0:T(8,128)(2,1)S(1)}, u32[]{:S(2)}, u32[]{:S(2)}) collective-permute-start(bf16[192,768]{1,0:T(8,128)(2,1)} %collective-permute-done.3), channel_id=1, source_target_pairs={{0,7},{1,0},{2,1},{3,2},{4,3},{5,4},{6,5},{7,6},{8,15},{9,8},{10,9... | collective-permute-start | bytes 884744 | tf_op jit(solution)/shard_map/ppermute | solution.py:15
  45.5 3.0 collective-permute-done.11
  48.5 3.3 %collective-permute-start.14 = (bf16[192,768]{1,0:T(8,128)(2,1)}, bf16[192,768]{1,0:T(8,128)(2,1)S(1)}, u32[]{:S(2)}, u32[]{:S(2)}) collective-permute-start(bf16[192,768]{1,0:T(8,128)(2,1)} %collective-permute-done.12), channel_id=1, source_target_pairs={{0,7},{1,0},{2,1},{3,2},{4,3},{5,4},{6,5},{7,6},{8,15},{9,8},{10,9... | collective-permute-start | bytes 884744 | tf_op jit(solution)/shard_map/ppermute | solution.py:15
  51.8 3.0 collective-permute-done.4
  56.2 3.2 %collective-permute-start.7 = (bf16[96,768]{1,0:T(8,128)(2,1)}, bf16[96,768]{1,0:T(8,128)(2,1)}, u32[]{:S(2)}, u32[]{:S(2)}) collective-permute-start(bf16[96,768]{1,0:T(8,128)(2,1)} %slice.17), channel_id=1, source_target_pairs={{0,7},{1,0},{2,1},{3,2},{4,3},{5,4},{6,5},{7,6},{8,15},{9,8},{10,9... | collective-permute-start | bytes 442376 | tf_op jit(solution)/shard_map/ppermute | solution.py:15
  59.4 1.5 collective-permute-done.13
  62.4 3.2 %collective-permute-start.16 = (bf16[96,768]{1,0:T(8,128)(2,1)}, bf16[96,768]{1,0:T(8,128)(2,1)}, u32[]{:S(2)}, u32[]{:S(2)}) collective-permute-start(bf16[96,768]{1,0:T(8,128)(2,1)} %slice.19), channel_id=1, source_target_pairs={{0,7},{1,0},{2,1},{3,2},{4,3},{5,4},{6,5},{7,6},{8,15},{9,8},{10,9... | collective-permute-start | bytes 442376 | tf_op jit(solution)/shard_map/ppermute | solution.py:15
  66.4 2.4 broadcast_in_dim.77
  68.8 11.7 %dynamic_update_slice.54 = bf16[16,192,768]{2,0,1:T(8,128)(2,1)} dynamic-update-slice(bf16[16,192,768]{2,0,1:T(8,128)(2,1)} %broadcast_in_dim.77, bf16[1,192,768]{2,0,1:T(2,128)(2,1)S(1)} %copy.26, s32[]{:T(128)S(6)} %select_n.108, s32[]{:T(128)} %constant.75.clone.1, s32[]{:T(128)} %constant.75.clone.1) | dynamic-update-slice | bytes 589828 | tf_op jit(solution)/shard_map/dynamic_update_slice | solution.py:37
  81.9 11.7 %dynamic_update_slice.55 = bf16[16,192,768]{2,0,1:T(8,128)(2,1)} dynamic-update-slice(bf16[16,192,768]{2,0,1:T(8,128)(2,1)} %dynamic_update_slice.54, bf16[1,192,768]{2,0,1:T(2,128)(2,1)S(1)} %copy.27, s32[]{:T(128)S(6)} %select_n.110, s32[]{:T(128)} %constant.75.clone.1, s32[]{:T(128)} %constant.75.clone.1) | dynamic-update-slice | bytes 589828 | tf_op jit(solution)/shard_map/dynamic_update_slice | solution.py:37
  93.6 11.7 %dynamic_update_slice.56 = bf16[16,192,768]{2,0,1:T(8,128)(2,1)} dynamic-update-slice(bf16[16,192,768]{2,0,1:T(8,128)(2,1)} %dynamic_update_slice.55, bf16[1,192,768]{2,0,1:T(2,128)(2,1)S(1)} %copy.28, s32[]{:T(128)S(6)} %select_n.112, s32[]{:T(128)} %constant.75.clone.1, s32[]{:T(128)} %constant.75.clone.1) | dynamic-update-slice | bytes 589828 | tf_op jit(solution)/shard_map/dynamic_update_slice | solution.py:37
  105.4 1.4 copy.29
  106.8 1.4 copy.30
  108.7 1.4 copy.37
  110.1 11.7 %dynamic_update_slice.57 = bf16[16,192,768]{2,0,1:T(8,128)(2,1)} dynamic-update-slice(bf16[16,192,768]{2,0,1:T(8,128)(2,1)} %dynamic_update_slice.56, bf16[1,192,768]{2,0,1:T(2,128)(2,1)S(1)} %copy.29, s32[]{:T(128)S(6)} %select_n.114, s32[]{:T(128)} %constant.75.clone.1, s32[]{:T(128)} %constant.75.clone.1) | dynamic-update-slice | bytes 589828 | tf_op jit(solution)/shard_map/dynamic_update_slice | solution.py:37
  121.8 11.7 %dynamic_update_slice.58 = bf16[16,192,768]{2,0,1:T(8,128)(2,1)} dynamic-update-slice(bf16[16,192,768]{2,0,1:T(8,128)(2,1)} %dynamic_update_slice.57, bf16[1,192,768]{2,0,1:T(2,128)(2,1)S(1)} %copy.30, s32[]{:T(128)S(6)} %select_n.116, s32[]{:T(128)} %constant.75.clone.1, s32[]{:T(128)} %constant.75.clone.1) | dynamic-update-slice | bytes 589828 | tf_op jit(solution)/shard_map/dynamic_update_slice | solution.py:37
  133.5 1.3 copy.31
  134.8 1.4 copy.32
  136.2 1.4 copy.38
  137.7 1.4 copy.39
  139.1 11.8 %dynamic_update_slice.59 = bf16[16,192,768]{2,0,1:T(8,128)(2,1)} dynamic-update-slice(bf16[16,192,768]{2,0,1:T(8,128)(2,1)} %dynamic_update_slice.58, bf16[1,192,768]{2,0,1:T(2,128)(2,1)} %copy.31, s32[]{:T(128)S(6)} %select_n.118, s32[]{:T(128)} %constant.75.clone.1, s32[]{:T(128)} %constant.75.clone.1) | dynamic-update-slice | bytes 589828 | tf_op jit(solution)/shard_map/dynamic_update_slice | solution.py:37
  150.8 11.7 %dynamic_update_slice.60 = bf16[16,192,768]{2,0,1:T(8,128)(2,1)} dynamic-update-slice(bf16[16,192,768]{2,0,1:T(8,128)(2,1)} %dynamic_update_slice.59, bf16[1,192,768]{2,0,1:T(2,128)(2,1)S(1)} %copy.32, s32[]{:T(128)S(6)} %select_n.120, s32[]{:T(128)} %constant.75.clone.1, s32[]{:T(128)} %constant.75.clone.1) | dynamic-update-slice | bytes 589828 | tf_op jit(solution)/shard_map/dynamic_update_slice | solution.py:37
  164.9 6.5 %dynamic_update_slice.61 = bf16[16,192,768]{2,0,1:T(8,128)(2,1)} dynamic-update-slice(bf16[16,192,768]{2,0,1:T(8,128)(2,1)} %dynamic_update_slice.60, bf16[1,96,768]{2,0,1:T(2,128)(2,1)S(1)} %copy.33, s32[]{:T(128)S(6)} %select_n.122, s32[]{:T(128)} %constant.75.clone.1, s32[]{:T(128)} %constant.75.clone.1) | dynamic-update-slice | bytes 294916 | tf_op jit(solution)/shard_map/dynamic_update_slice | solution.py:37
  171.4 6.5 %dynamic_update_slice.62 = bf16[16,192,768]{2,0,1:T(8,128)(2,1)} dynamic-update-slice(bf16[16,192,768]{2,0,1:T(8,128)(2,1)} %dynamic_update_slice.61, bf16[1,96,768]{2,0,1:T(2,128)(2,1)S(1)} %copy.34, s32[]{:T(128)S(6)} %select_n.122, s32[]{:T(128)} %constant.86.clone.1, s32[]{:T(128)} %constant.75.clone.1) | dynamic-update-slice | bytes 294916 | tf_op jit(solution)/shard_map/dynamic_update_slice | solution.py:37
  177.9 11.8 %dynamic_update_slice.63 = bf16[16,192,768]{2,0,1:T(8,128)(2,1)} dynamic-update-slice(bf16[16,192,768]{2,0,1:T(8,128)(2,1)} %dynamic_update_slice.62, bf16[1,192,768]{2,0,1:T(2,128)(2,1)S(1)} %copy.35, s32[]{:T(128)S(6)} %select_n.123, s32[]{:T(128)} %constant.75.clone.1, s32[]{:T(128)} %constant.75.clone.1) | dynamic-update-slice | bytes 589828 | tf_op jit(solution)/shard_map/dynamic_update_slice | solution.py:37
  189.7 11.7 %dynamic_update_slice.64 = bf16[16,192,768]{2,0,1:T(8,128)(2,1)} dynamic-update-slice(bf16[16,192,768]{2,0,1:T(8,128)(2,1)} %dynamic_update_slice.63, bf16[1,192,768]{2,0,1:T(2,128)(2,1)S(1)} %copy.36, s32[]{:T(128)S(6)} %select_n.124, s32[]{:T(128)} %constant.75.clone.1, s32[]{:T(128)} %constant.75.clone.1) | dynamic-update-slice | bytes 589828 | tf_op jit(solution)/shard_map/dynamic_update_slice | solution.py:37
  201.4 11.7 %dynamic_update_slice.65 = bf16[16,192,768]{2,0,1:T(8,128)(2,1)} dynamic-update-slice(bf16[16,192,768]{2,0,1:T(8,128)(2,1)} %dynamic_update_slice.64, bf16[1,192,768]{2,0,1:T(2,128)(2,1)S(1)} %copy.37, s32[]{:T(128)S(6)} %select_n.125, s32[]{:T(128)} %constant.75.clone.1, s32[]{:T(128)} %constant.75.clone.1) | dynamic-update-slice | bytes 589828 | tf_op jit(solution)/shard_map/dynamic_update_slice | solution.py:37
  213.1 11.7 %dynamic_update_slice.66 = bf16[16,192,768]{2,0,1:T(8,128)(2,1)} dynamic-update-slice(bf16[16,192,768]{2,0,1:T(8,128)(2,1)} %dynamic_update_slice.65, bf16[1,192,768]{2,0,1:T(2,128)(2,1)S(1)} %copy.38, s32[]{:T(128)S(6)} %select_n.126, s32[]{:T(128)} %constant.75.clone.1, s32[]{:T(128)} %constant.75.clone.1) | dynamic-update-slice | bytes 589828 | tf_op jit(solution)/shard_map/dynamic_update_slice | solution.py:37
  224.8 11.7 %dynamic_update_slice.67 = bf16[16,192,768]{2,0,1:T(8,128)(2,1)} dynamic-update-slice(bf16[16,192,768]{2,0,1:T(8,128)(2,1)} %dynamic_update_slice.66, bf16[1,192,768]{2,0,1:T(2,128)(2,1)S(1)} %copy.39, s32[]{:T(128)S(6)} %select_n.127, s32[]{:T(128)} %constant.75.clone.1, s32[]{:T(128)} %constant.75.clone.1) | dynamic-update-slice | bytes 589828 | tf_op jit(solution)/shard_map/dynamic_update_slice | solution.py:37
  237.5 11.7 %dynamic_update_slice.68 = bf16[16,192,768]{2,0,1:T(8,128)(2,1)} dynamic-update-slice(bf16[16,192,768]{2,0,1:T(8,128)(2,1)} %dynamic_update_slice.67, bf16[1,192,768]{2,0,1:T(2,128)(2,1)S(1)} %copy.40, s32[]{:T(128)S(6)} %select_n.128, s32[]{:T(128)} %constant.75.clone.1, s32[]{:T(128)} %constant.75.clone.1) | dynamic-update-slice | bytes 589828 | tf_op jit(solution)/shard_map/dynamic_update_slice | solution.py:37
  249.2 11.7 %dynamic_update_slice.69 = bf16[16,192,768]{2,0,1:T(8,128)(2,1)} dynamic-update-slice(bf16[16,192,768]{2,0,1:T(8,128)(2,1)} %dynamic_update_slice.68, bf16[1,192,768]{2,0,1:T(2,128)(2,1)S(1)} %copy.41, s32[]{:T(128)S(6)} %select_n.129, s32[]{:T(128)} %constant.75.clone.1, s32[]{:T(128)} %constant.75.clone.1) | dynamic-update-slice | bytes 589828 | tf_op jit(solution)/shard_map/dynamic_update_slice | solution.py:37
  262.1 1.1 copy.43
  263.3 6.5 %dynamic_update_slice.70 = bf16[16,192,768]{2,0,1:T(8,128)(2,1)} dynamic-update-slice(bf16[16,192,768]{2,0,1:T(8,128)(2,1)} %dynamic_update_slice.69, bf16[1,96,768]{2,0,1:T(2,128)(2,1)S(1)} %copy.42, s32[]{:T(128)S(6)} %select_n.130, s32[]{:T(128)} %constant.75.clone.1, s32[]{:T(128)} %constant.75.clone.1) | dynamic-update-slice | bytes 294916 | tf_op jit(solution)/shard_map/dynamic_update_slice | solution.py:37
  269.8 6.5 %dynamic_update_slice.71 = bf16[16,192,768]{2,0,1:T(8,128)(2,1)} dynamic-update-slice(bf16[16,192,768]{2,0,1:T(8,128)(2,1)} %dynamic_update_slice.70, bf16[1,96,768]{2,0,1:T(2,128)(2,1)S(1)} %copy.43, s32[]{:T(128)S(6)} %select_n.130, s32[]{:T(128)} %constant.86.clone.1, s32[]{:T(128)} %constant.75.clone.1) | dynamic-update-slice | bytes 294916 | tf_op jit(solution)/shard_map/dynamic_update_slice | solution.py:37
  276.2 7.2 %copy.44 = bf16[16,16,12,768]{3,2,1,0:T(8,128)(2,1)} copy(bf16[16,16,12,768]{3,1,2,0:T(8,128)(2,1)} %bitcast.28) | data formatting | bytes 9437184 | tf_op jit(solution)/shard_map/transpose | solution.py:54
  283.4 8.5 %reshape.18 = bf16[3072,768]{1,0:T(8,128)(2,1)} reshape(bf16[16,16,12,768]{3,2,1,0:T(8,128)(2,1)} %copy.44) | data formatting | bytes 9437184 | tf_op jit(solution)/shard_map/reshape | solution.py:54
  291.9 12.8 %add_convert_fusion = bf16[768,1536]{1,0:T(8,128)(2,1)} fusion(bf16[768,1536]{1,0:T(8,128)(2,1)S(1)} %copy-done.11, bf16[3072,768]{1,0:T(8,128)(2,1)} %reshape.18, bf16[3072,1536]{1,0:T(8,128)(2,1)} %all-gather.2.cloned.1.call-done, s32[1536]{0:T(1024)S(1)} %eq.47, s32[768]{0:T(1024)S(1)} %eq.45), kind=kOutput, calls=%fused_computation | convolution fusion | flops 7253655552 | bytes 18883584 | tf_op jit(solution)/shard_map/dot_general | solution.py:56
  (68 shorter events, 13.5 us)
Async XLA Ops:
  6.5 59.1 %copy-start = (bf16[768,192]{0,1:T(8,128)(2,1)S(1)}, bf16[768,192]{0,1:T(8,128)(2,1)}, u32[]{:S(2)}) copy-start(bf16[768,192]{0,1:T(8,128)(2,1)} %param.6) | copy-start | bytes 884740
  6.5 59.7 %copy-start.10 = (s32[16]{0:T(128)S(1)}, s32[16]{0:T(128)}, u32[]{:S(2)}) copy-start(s32[16]{0:T(128)} %param.11) | copy-start | bytes 196
  6.5 285.4 %all-gather.2.cloned.1.call-start = ((), (), s32[]{:S(2)}) async-start(), calls=%async_computation | async-start | bytes 10027008 | tf_op jit(solution)/shard_map/all_gather | solution.py:50
  11.7 10.3 %collective-permute-start.8 = (bf16[192,768]{1,0:T(8,128)(2,1)S(1)}, bf16[192,768]{1,0:T(8,128)(2,1)S(1)}, u32[]{:S(2)}, u32[]{:S(2)}) collective-permute-start(bf16[192,768]{1,0:T(8,128)(2,1)S(1)} %compare_select_fusion), channel_id=1, source_target_pairs={{0,8},{8,0},{1,9},{9,1},{2,10},{10,2},{3,11},{11,3},{4,12},{12,4},... | collective-permute-start | bytes 884744 | tf_op jit(solution)/shard_map/ppermute | solution.py:15
  14.1 13.8 %collective-permute-start = (bf16[192,768]{1,0:T(8,128)(2,1)S(1)}, bf16[192,768]{1,0:T(8,128)(2,1)S(1)}, u32[]{:S(2)}, u32[]{:S(2)}) collective-permute-start(bf16[192,768]{1,0:T(8,128)(2,1)S(1)} %compare_select_fusion), channel_id=1, source_target_pairs={{0,1},{1,2},{2,3},{3,4},{4,5},{5,6},{6,7},{7,0},{8,9},{9,10},{10,1... | collective-permute-start | bytes 884744 | tf_op jit(solution)/shard_map/ppermute | solution.py:15
  16.0 11.9 %collective-permute-start.1 = (bf16[192,768]{1,0:T(8,128)(2,1)S(1)}, bf16[192,768]{1,0:T(8,128)(2,1)S(1)}, u32[]{:S(2)}, u32[]{:S(2)}) collective-permute-start(bf16[192,768]{1,0:T(8,128)(2,1)S(1)} %compare_select_fusion), channel_id=1, source_target_pairs={{0,7},{1,0},{2,1},{3,2},{4,3},{5,4},{6,5},{7,6},{8,15},{9,8},{10,9... | collective-permute-start | bytes 884744 | tf_op jit(solution)/shard_map/ppermute | solution.py:15
  22.1 13.8 %collective-permute-start.9 = (bf16[192,768]{1,0:T(8,128)(2,1)S(1)}, bf16[192,768]{1,0:T(8,128)(2,1)S(1)}, u32[]{:S(2)}, u32[]{:S(2)}) collective-permute-start(bf16[192,768]{1,0:T(8,128)(2,1)S(1)} %collective-permute-done.8), channel_id=1, source_target_pairs={{0,1},{1,2},{2,3},{3,4},{4,5},{5,6},{6,7},{7,0},{8,9},{9,10},{10,1... | collective-permute-start | bytes 884744 | tf_op jit(solution)/shard_map/ppermute | solution.py:15
  24.0 11.9 %collective-permute-start.10 = (bf16[192,768]{1,0:T(8,128)(2,1)S(1)}, bf16[192,768]{1,0:T(8,128)(2,1)S(1)}, u32[]{:S(2)}, u32[]{:S(2)}) collective-permute-start(bf16[192,768]{1,0:T(8,128)(2,1)S(1)} %collective-permute-done.8), channel_id=1, source_target_pairs={{0,7},{1,0},{2,1},{3,2},{4,3},{5,4},{6,5},{7,6},{8,15},{9,8},{10,9... | collective-permute-start | bytes 884744 | tf_op jit(solution)/shard_map/ppermute | solution.py:15
  27.9 14.3 %collective-permute-start.2 = (bf16[192,768]{1,0:T(8,128)(2,1)S(1)}, bf16[192,768]{1,0:T(8,128)(2,1)}, u32[]{:S(2)}, u32[]{:S(2)}) collective-permute-start(bf16[192,768]{1,0:T(8,128)(2,1)S(1)} %collective-permute-done), channel_id=1, source_target_pairs={{0,1},{1,2},{2,3},{3,4},{4,5},{5,6},{6,7},{7,0},{8,9},{9,10},{10,1... | collective-permute-start | bytes 884744 | tf_op jit(solution)/shard_map/ppermute | solution.py:15
  28.0 14.3 %collective-permute-start.3 = (bf16[192,768]{1,0:T(8,128)(2,1)S(1)}, bf16[192,768]{1,0:T(8,128)(2,1)}, u32[]{:S(2)}, u32[]{:S(2)}) collective-permute-start(bf16[192,768]{1,0:T(8,128)(2,1)S(1)} %collective-permute-done.1), channel_id=1, source_target_pairs={{0,7},{1,0},{2,1},{3,2},{4,3},{5,4},{6,5},{7,6},{8,15},{9,8},{10,9... | collective-permute-start | bytes 884744 | tf_op jit(solution)/shard_map/ppermute | solution.py:15
  35.9 44.6 %copy-start.6 = (bf16[192,768]{1,0:T(8,128)(2,1)}, bf16[192,768]{1,0:T(8,128)(2,1)S(1)}, u32[]{:S(2)}) copy-start(bf16[192,768]{1,0:T(8,128)(2,1)S(1)} %collective-permute-done.9) | copy-start | bytes 884740
  35.9 12.6 %collective-permute-start.11 = (bf16[192,768]{1,0:T(8,128)(2,1)S(1)}, bf16[192,768]{1,0:T(8,128)(2,1)S(1)}, u32[]{:S(2)}, u32[]{:S(2)}) collective-permute-start(bf16[192,768]{1,0:T(8,128)(2,1)S(1)} %collective-permute-done.9), channel_id=1, source_target_pairs={{0,1},{1,2},{2,3},{3,4},{4,5},{5,6},{6,7},{7,0},{8,9},{9,10},{10,1... | collective-permute-start | bytes 884744 | tf_op jit(solution)/shard_map/ppermute | solution.py:15
  35.9 44.6 %copy-start.8 = (bf16[192,768]{1,0:T(8,128)(2,1)}, bf16[192,768]{1,0:T(8,128)(2,1)S(1)}, u32[]{:S(2)}) copy-start(bf16[192,768]{1,0:T(8,128)(2,1)S(1)} %collective-permute-done.10) | copy-start | bytes 884740
  35.9 12.6 %collective-permute-start.12 = (bf16[192,768]{1,0:T(8,128)(2,1)S(1)}, bf16[192,768]{1,0:T(8,128)(2,1)}, u32[]{:S(2)}, u32[]{:S(2)}) collective-permute-start(bf16[192,768]{1,0:T(8,128)(2,1)S(1)} %collective-permute-done.10), channel_id=1, source_target_pairs={{0,7},{1,0},{2,1},{3,2},{4,3},{5,4},{6,5},{7,6},{8,15},{9,8},{10,9... | collective-permute-start | bytes 884744 | tf_op jit(solution)/shard_map/ppermute | solution.py:15
  42.3 12.5 %collective-permute-start.4 = (bf16[192,768]{1,0:T(8,128)(2,1)}, bf16[192,768]{1,0:T(8,128)(2,1)S(1)}, u32[]{:S(2)}, u32[]{:S(2)}) collective-permute-start(bf16[192,768]{1,0:T(8,128)(2,1)} %collective-permute-done.2), channel_id=1, source_target_pairs={{0,1},{1,2},{2,3},{3,4},{4,5},{5,6},{6,7},{7,0},{8,9},{9,10},{10,1... | collective-permute-start | bytes 884744 | tf_op jit(solution)/shard_map/ppermute | solution.py:15
  42.3 13.2 %collective-permute-start.5 = (bf16[192,768]{1,0:T(8,128)(2,1)}, bf16[192,768]{1,0:T(8,128)(2,1)S(1)}, u32[]{:S(2)}, u32[]{:S(2)}) collective-permute-start(bf16[192,768]{1,0:T(8,128)(2,1)} %collective-permute-done.3), channel_id=1, source_target_pairs={{0,7},{1,0},{2,1},{3,2},{4,3},{5,4},{6,5},{7,6},{8,15},{9,8},{10,9... | collective-permute-start | bytes 884744 | tf_op jit(solution)/shard_map/ppermute | solution.py:15
  48.5 58.3 %copy-start.9 = (bf16[192,768]{1,0:T(8,128)(2,1)}, bf16[192,768]{1,0:T(8,128)(2,1)S(1)}, u32[]{:S(2)}) copy-start(bf16[192,768]{1,0:T(8,128)(2,1)S(1)} %collective-permute-done.11) | copy-start | bytes 884740
  48.5 12.4 %collective-permute-start.13 = (bf16[192,768]{1,0:T(8,128)(2,1)S(1)}, bf16[192,768]{1,0:T(8,128)(2,1)S(1)}, u32[]{:S(2)}, u32[]{:S(2)}) collective-permute-start(bf16[192,768]{1,0:T(8,128)(2,1)S(1)} %collective-permute-done.11), channel_id=1, source_target_pairs={{0,1},{1,2},{2,3},{3,4},{4,5},{5,6},{6,7},{7,0},{8,9},{9,10},{10,1... | collective-permute-start | bytes 884744 | tf_op jit(solution)/shard_map/ppermute | solution.py:15
  48.5 13.1 %collective-permute-start.14 = (bf16[192,768]{1,0:T(8,128)(2,1)}, bf16[192,768]{1,0:T(8,128)(2,1)S(1)}, u32[]{:S(2)}, u32[]{:S(2)}) collective-permute-start(bf16[192,768]{1,0:T(8,128)(2,1)} %collective-permute-done.12), channel_id=1, source_target_pairs={{0,7},{1,0},{2,1},{3,2},{4,3},{5,4},{6,5},{7,6},{8,15},{9,8},{10,9... | collective-permute-start | bytes 884744 | tf_op jit(solution)/shard_map/ppermute | solution.py:15
  55.5 107.1 %collective-permute-start.6 = (bf16[96,768]{1,0:T(8,128)(2,1)}, bf16[96,768]{1,0:T(8,128)(2,1)}, u32[]{:S(2)}, u32[]{:S(2)}) collective-permute-start(bf16[96,768]{1,0:T(8,128)(2,1)} %slice.16), channel_id=1, source_target_pairs={{0,1},{1,2},{2,3},{3,4},{4,5},{5,6},{6,7},{7,0},{8,9},{9,10},{10,1... | collective-permute-start | bytes 442376 | tf_op jit(solution)/shard_map/ppermute | solution.py:15
  55.5 25.9 %copy-start.5 = (bf16[192,768]{1,0:T(8,128)(2,1)}, bf16[192,768]{1,0:T(8,128)(2,1)S(1)}, u32[]{:S(2)}) copy-start(bf16[192,768]{1,0:T(8,128)(2,1)S(1)} %collective-permute-done.5) | copy-start | bytes 884740
  56.2 107.5 %collective-permute-start.7 = (bf16[96,768]{1,0:T(8,128)(2,1)}, bf16[96,768]{1,0:T(8,128)(2,1)}, u32[]{:S(2)}, u32[]{:S(2)}) collective-permute-start(bf16[96,768]{1,0:T(8,128)(2,1)} %slice.17), channel_id=1, source_target_pairs={{0,7},{1,0},{2,1},{3,2},{4,3},{5,4},{6,5},{7,6},{8,15},{9,8},{10,9... | collective-permute-start | bytes 442376 | tf_op jit(solution)/shard_map/ppermute | solution.py:15
  60.9 4.7 %copy-start.1 = (bf16[192,768]{1,0:T(8,128)(2,1)}, bf16[192,768]{1,0:T(8,128)(2,1)S(1)}, u32[]{:S(2)}) copy-start(bf16[192,768]{1,0:T(8,128)(2,1)S(1)} %collective-permute-done.13) | copy-start | bytes 884740
  61.6 199.3 %collective-permute-start.15 = (bf16[96,768]{1,0:T(8,128)(2,1)}, bf16[96,768]{1,0:T(8,128)(2,1)}, u32[]{:S(2)}, u32[]{:S(2)}) collective-permute-start(bf16[96,768]{1,0:T(8,128)(2,1)} %slice.18), channel_id=1, source_target_pairs={{0,1},{1,2},{2,3},{3,4},{4,5},{5,6},{6,7},{7,0},{8,9},{9,10},{10,1... | collective-permute-start | bytes 442376 | tf_op jit(solution)/shard_map/ppermute | solution.py:15
  61.6 4.0 %copy-start.3 = (bf16[192,768]{1,0:T(8,128)(2,1)}, bf16[192,768]{1,0:T(8,128)(2,1)S(1)}, u32[]{:S(2)}) copy-start(bf16[192,768]{1,0:T(8,128)(2,1)S(1)} %collective-permute-done.14) | copy-start | bytes 884740
  62.4 199.8 %collective-permute-start.16 = (bf16[96,768]{1,0:T(8,128)(2,1)}, bf16[96,768]{1,0:T(8,128)(2,1)}, u32[]{:S(2)}, u32[]{:S(2)}) collective-permute-start(bf16[96,768]{1,0:T(8,128)(2,1)} %slice.19), channel_id=1, source_target_pairs={{0,7},{1,0},{2,1},{3,2},{4,3},{5,4},{6,5},{7,6},{8,15},{9,8},{10,9... | collective-permute-start | bytes 442376 | tf_op jit(solution)/shard_map/ppermute | solution.py:15
  81.4 26.8 %copy-start.7 = (bf16[192,768]{1,0:T(8,128)(2,1)S(1)}, bf16[192,768]{1,0:T(8,128)(2,1)}, u32[]{:S(2)}) copy-start(bf16[192,768]{1,0:T(8,128)(2,1)} %copy-done.6) | copy-start | bytes 884740
  171.4 65.2 %copy-start.2 = (bf16[192,768]{1,0:T(8,128)(2,1)S(1)}, bf16[192,768]{1,0:T(8,128)(2,1)}, u32[]{:S(2)}) copy-start(bf16[192,768]{1,0:T(8,128)(2,1)} %copy-done.1) | copy-start | bytes 884740
  177.9 59.1 %copy-start.4 = (bf16[192,768]{1,0:T(8,128)(2,1)S(1)}, bf16[192,768]{1,0:T(8,128)(2,1)}, u32[]{:S(2)}) copy-start(bf16[192,768]{1,0:T(8,128)(2,1)} %copy-done.3) | copy-start | bytes 884740
  283.4 8.5 %copy-start.11 = (bf16[768,1536]{1,0:T(8,128)(2,1)S(1)}, bf16[768,1536]{1,0:T(8,128)(2,1)}, u32[]{:S(2)}) copy-start(bf16[768,1536]{1,0:T(8,128)(2,1)} %param.8) | copy-start | bytes 7077892
Sparse Core Ops, SparseCore 0:
  9.2 62.1 all-gather.1

commit v2 on v1

v2 whole, which is shorter than its diff:
```python
import functools

import jax
import jax.numpy as jnp
from jax import lax
from jax.experimental import pallas as pl
from jax.experimental.pallas import tpu as pltpu
from jax.sharding import Mesh, PartitionSpec as P

TILE = 96
FINE = ("ylo", "x", "core", "yhi", "z")
ROW = ("ylo", "x", "core")
COL = ("yhi", "z")


def shift(value, axis, steps):
    count = lax.axis_size(axis)
    return lax.ppermute(value, axis, [(i, (i + steps) % count) for i in range(count)])


def after(values, earlier):
    return lax.optimization_barrier((tuple(values), tuple(earlier)))[0]


def ring(own):
    count = lax.axis_size("z")
    other = shift(own, "yhi", 1)
    found = [(own, 0, 0), (other, 1, 0)]
    ends = [(own, own), (other, other)]
    for step in range(1, count // 2):
        for plane in (0, 1):
            up, down = ends[plane]
            up, down = ends[plane] = (shift(up, "z", 1), shift(down, "z", -1))
            found += [(up, plane, -step), (down, plane, step)]
    for plane, way in ((0, 1), (1, -1)):
        (last,) = after(ends[plane][plane : plane + 1], ends[plane])
        found.append((shift(last, "z", way), plane, count // 2))
    return found


def mask_kernel(pair_ref, cd_ref, amp_ref, out_ref):
    group = lax.axis_index("yhi") * lax.axis_size("z") + lax.axis_index("z")
    column = lax.broadcasted_iota(jnp.int32, (1, amp_ref.shape[1]), 1)
    labels = jnp.full(column.shape, pair_ref[0])
    for tile in range(1, pair_ref.shape[0]):
        labels = jnp.where(column >= tile * TILE, pair_ref[tile], labels)
    for tile in range(amp_ref.shape[0] // TILE):
        rows = slice(tile * TILE, (tile + 1) * TILE)
        kept = labels == cd_ref[group * 2 + tile]
        out_ref[rows] = jnp.where(kept, amp_ref[rows].astype(jnp.float32), 0.0).astype(out_ref.dtype)


def masked(amplitudes, pair_class, cd_class):
    smem = pl.BlockSpec(memory_space=pltpu.SMEM)
    vmem = pl.BlockSpec(memory_space=pltpu.VMEM)
    return pl.pallas_call(
        mask_kernel,
        out_shape=jax.ShapeDtypeStruct(amplitudes.shape, amplitudes.dtype),
        in_specs=[smem, smem, vmem],
        out_specs=vmem,
        compiler_params=pltpu.CompilerParams(vmem_limit_bytes=24 << 20),
        name="mask_amplitudes",
    )(pair_class, cd_class, amplitudes)


def ordered(integrals, order):
    groups, part, width = integrals.shape
    flat = integrals.transpose(1, 0, 2).reshape(part * groups, width)
    place = jnp.arange(part, dtype=jnp.int32)[None, :] * groups + order[:, None]
    chosen = place.reshape(-1, 1) == jnp.arange(part * groups, dtype=jnp.int32)[None, :]
    return jnp.dot(chosen.astype(integrals.dtype), flat, preferred_element_type=jnp.float32).astype(integrals.dtype)


def arrange(chunk_refs, out_ref):
    wide, part = 128, 12

    @pl.loop(0, out_ref.shape[0] // wide)
    def _(step):
        lanes = pl.ds(pl.multiple_of(step * wide, wide), wide)
        size = out_ref.shape[1] // 4
        for quad in range(4):
            pieces = [[], [], [], []]
            for pair in (0, 2):
                at = (quad * 4 + pair) * part
                for chunk in chunk_refs:
                    both = chunk[at : at + 2 * part, lanes].astype(jnp.float32)
                    pieces[pair].append(both[:part])
                    pieces[pair + 1].append(both[part:])
            block = jnp.concatenate(sum(pieces, []))
            out_ref[lanes, quad * size : (quad + 1) * size] = block.T.astype(out_ref.dtype)


def arranged(chunks):
    deep, wide = chunks[0].shape
    return pl.pallas_call(
        lambda *refs: arrange(refs[:-1], refs[-1]),
        out_shape=jax.ShapeDtypeStruct((wide, len(chunks) * deep), chunks[0].dtype),
        in_specs=[pl.BlockSpec(memory_space=pltpu.VMEM)] * len(chunks),
        out_specs=pl.BlockSpec(memory_space=pltpu.VMEM),
        compiler_params=pltpu.CompilerParams(vmem_limit_bytes=24 << 20),
        cost_estimate=pl.CostEstimate(flops=10**8, bytes_accessed=10**7, transcendentals=0),
        name="arrange_amplitudes",
    )(*chunks)


def product_kernel(block, pair_ref, ab_ref, early_ref, late_ref, panel_ref, prior_ref, out_ref, late, held, prior, done, late_sem, sems):
    in_sem, prior_sem, out_sem = (sems.at[i] for i in range(3))
    deep, half = early_ref.shape[1], panel_ref.shape[1] // 2
    steps = out_ref.shape[1] // block

    def columns(step):
        return pl.ds(pl.multiple_of(step * block, block), block)

    def fetch(step):
        return pltpu.make_async_copy(panel_ref.at[:, :, columns(step)], held.at[:, :, columns(step)], in_sem.at[step])

    def put(step):
        return pltpu.make_async_copy(done.at[:, columns(step)], out_ref.at[:, columns(step)], out_sem.at[step])

    def fetch_prior(step):
        return pltpu.make_async_copy(prior_ref.at[:, columns(step)], prior.at[:, columns(step)], prior_sem.at[step])

    fetch_late = pltpu.make_async_copy(late_ref, late, late_sem)
    fetch_late.start()
    for step in range(steps):
        fetch(step).start()
        fetch_prior(step).start()
    fetch_late.wait()

    @pl.loop(0, steps)
    def _(step):
        fetch(step).wait()
        lanes = columns(step)
        column = step * block + lax.broadcasted_iota(jnp.int32, (1, block), 1)
        labels = jnp.full((1, block), ab_ref[0])
        for tile in range(1, ab_ref.shape[0]):
            labels = jnp.where(column >= tile * TILE, ab_ref[tile], labels)
        ladder = sum(
            jnp.dot(amp[...], held[:, at : at + half, lanes].reshape(deep, block), preferred_element_type=jnp.float32)
            for amp, at in ((early_ref, 0), (late, half))
        )
        fetch_prior(step).wait()
        for tile in range(out_ref.shape[0] // TILE):
            rows = slice(tile * TILE, (tile + 1) * TILE)
            kept = jnp.where(labels == pair_ref[tile], ladder[rows], 0.0)
            done[rows, lanes] = (prior[rows, lanes].astype(jnp.float32) + kept).astype(done.dtype)
        put(step).start()

    for step in range(steps):
        put(step).wait()


def finished(early, late, panel, prior, pair_class, ab_class):
    high, deep = early.shape
    width = panel.shape[2]
    block = 256
    steps = width // block
    smem, vmem = (pl.BlockSpec(memory_space=space) for space in (pltpu.SMEM, pltpu.VMEM))
    hbm = pl.BlockSpec(memory_space=pltpu.HBM)
    keep = pltpu.with_memory_space_constraint
    return pl.pallas_call(
        functools.partial(product_kernel, block),
        out_shape=jax.ShapeDtypeStruct(prior.shape, prior.dtype),
        in_specs=[smem, smem, vmem, hbm, hbm, hbm],
        out_specs=hbm,
        scratch_shapes=[
            pltpu.VMEM(late.shape, late.dtype),
            pltpu.VMEM(panel.shape, panel.dtype),
            pltpu.VMEM(prior.shape, prior.dtype),
            pltpu.VMEM(prior.shape, prior.dtype),
            pltpu.SemaphoreType.DMA,
            pltpu.SemaphoreType.DMA((3, steps)),
        ],
        compiler_params=pltpu.CompilerParams(vmem_limit_bytes=24 << 20),
        cost_estimate=pl.CostEstimate(flops=4 * high * deep * width, bytes_accessed=4 * deep * width, transcendentals=0),
        name="product",
    )(pair_class, ab_class, keep(early, pltpu.VMEM), keep(late, pltpu.HBM), keep(panel, pltpu.HBM), keep(prior, pltpu.HBM))


def local(amplitudes, integrals, residual_in, pair_class, cd_class, ab_class):
    count = lax.axis_size("z")
    z, side = lax.axis_index("z"), lax.axis_index("yhi")
    found = ring(masked(amplitudes.T, pair_class, cd_class))
    order = jnp.stack([(side ^ plane) * count + (z + step) % count for _, plane, step in found])
    panel = lax.all_gather(ordered(integrals, order), ROW, axis=0)
    half = len(found) // 2
    chunks = [chunk for chunk, _, _ in found]
    return finished(arranged(chunks[:half]), arranged(chunks[half:]), panel, residual_in, pair_class, ab_class)


def solution(mesh):
    fine = Mesh(mesh.devices.reshape(2, 4, 2, 2, 8), FINE)
    return jax.shard_map(
        local,
        mesh=fine,
        in_specs=(P(ROW, COL), P(None, ROW, COL), P(ROW, COL), P(ROW), P(), P(COL)),
        out_specs=P(ROW, COL),
        check_vma=False,
    )
```

time: 317 us -> 96.1 us (0.30); the launches traced: 312 us -> 95.9 us
  local copies, waits for them, and re-layouts: 233 us -> 4.65 us
  Pallas kernels: 0 us -> 18.3 us
  waiting for transfers between devices: 17.4 us -> 29.8 us
  matrix products: 12.8 us -> 1.17 us
  starting transfers between devices: 33.6 us -> 28.4 us
    dynamic_update_slice x18 -> x0, local copies, waits for them, and re-layouts: 190 us -> none  [gather_amp(): lax.dynamic_update_slice(whole, chunk[None], (plane * count + place, row,...]
    broadcast_in_dim x22 -> x0, local copies, waits for them, and re-layouts: 21.4 us -> none  [the longest x18 17.5 us: gather_amp(): chunk[None]]
    pallas_call x0 -> x4, Pallas kernels: none -> 18.3 us  [the longest x1 15.5 us: finished(): pl.pallas_call(functools.partial(product_kernel, block), out_shape=jax.Sh...]
    ppermute x17 -> x15, waiting for transfers between devices: 17.4 us -> 29.8 us  [shift(): lax.ppermute(value, axis, [(i, (i + steps) % count) for i in range(count)])]
    dot_general x1, matrix products: 12.8 us -> 1.17 us  [ordered(): jnp.dot(chosen.astype(integrals.dtype), flat, preferred_element_type=jnp....]
    reshape x3 -> x0, local copies, waits for them, and re-layouts: 9.55 us -> none  [the longest x1 8.54 us: local(): whole.reshape(groups, rows, part, -1).transpose(1, 0, 2, 3)]
    transpose x1 -> x0, local copies, waits for them, and re-layouts: 7.15 us -> none  [local(): whole.reshape(groups, rows, part, -1).transpose(1, 0, 2, 3)]
    ppermute x17 -> x15, starting transfers between devices: 33.6 us -> 28.4 us  [shift(): lax.ppermute(value, axis, [(i, (i + steps) % count) for i in range(count)])]
  transfers between devices with their start and end apart: 18 -> 16, of which waited for: 6 -> 10; matrix products, arithmetic and copies ran while one was open for 74% -> 0% of each run, Pallas kernels for 0% -> 3%
where the time goes in v2:
time: 96.1 us; the launch traced here: 95.9 us
  waiting for transfers between devices  29.8 us (31%)
  starting transfers between devices  28.4 us (30%)
  Pallas kernels  18.3 us (19%)
  between operations  13.5 us (14%)
  local copies, waits for them, and re-layouts  4.65 us (5%)
  matrix products  1.17 us (1%)
    ppermute x15, waiting for transfers between devices, shift(): lax.ppermute(value, axis, [(i, (i + steps) % count) for i in range(count)])  29.8 us
    ppermute x15, starting transfers between devices, shift(): lax.ppermute(value, axis, [(i, (i + steps) % count) for i in range(count)])  28.4 us
    pallas_call x1, Pallas kernels, finished(): pl.pallas_call(functools.partial(product_kernel, block), out_shape=jax.Sh...  15.5 us
    unnamed x14, local copies, waits for them, and re-layouts  4.46 us
    pallas_call x2, Pallas kernels, arranged(): pl.pallas_call(lambda *refs: arrange(refs[:-1], refs[-1]), out_shape=jax....  2.14 us
  transfers between devices with their start and end apart: 16, of which 10 were waited for; matrix products, arithmetic and copies ran while one was open for 0% of the time, Pallas kernels for 3%

profile of v2, /device:TPU:12, one launch (start us, length us, event | category | flops | bytes accessed | tf_op | source)
XLA Modules:
  0.0 95.9 jit_solution(14583421795563321370)
XLA Ops:
  6.5 0.1 stack.67
  6.6 0.1 broadcast_add_fusion
  6.7 0.1 add.163
  6.8 0.8 copy-done
  7.6 1.2 %convolution_convert_fusion = bf16[192,1536]{1,0:T(8,128)(2,1)} fusion(bf16[192,1536]{1,0:T(8,128)(2,1)S(1)} %bitcast.22, s32[192]{0:T(256)S(1)} %add.163), kind=kOutput, calls=%fused_computation | convolution fusion | flops 113577984 | bytes 1180416 | tf_op jit(solution)/shard_map/dot_general | solution.py:71
  8.8 0.0 all-gather.3.cloned.1.call-update
  8.8 0.0 copy-start.2
  8.8 1.0 copy-done.2
  9.8 0.7 copy-done.3
  10.4 0.7 copy-done.4
  11.1 0.6 mask_amplitudes.1.refs_0_
  11.7 2.4 %collective-permute-start = (bf16[192,768]{1,0:T(8,128)(2,1)S(1)}, bf16[192,768]{1,0:T(8,128)(2,1)S(1)}, u32[]{:S(2)}, u32[]{:S(2)}) collective-permute-start(bf16[192,768]{1,0:T(8,128)(2,1)S(1)} %mask_amplitudes.1.refs_0_), channel_id=1, source_target_pairs={{0,8},{8,0},{1,9},{9,1},{2,10},{10,2},{3,11},{11,3},{4,12},{12,4},... | collective-permute-start | bytes 884744 | tf_op jit(solution)/shard_map/ppermute | solution.py:18
  14.1 5.9 %collective-permute-start.2 = (bf16[192,768]{1,0:T(8,128)(2,1)S(1)}, bf16[192,768]{1,0:T(8,128)(2,1)S(1)}, u32[]{:S(2)}, u32[]{:S(2)}) collective-permute-start(bf16[192,768]{1,0:T(8,128)(2,1)S(1)} %mask_amplitudes.1.refs_0_), channel_id=1, source_target_pairs={{0,7},{1,0},{2,1},{3,2},{4,3},{5,4},{6,5},{7,6},{8,15},{9,8},{10,9... | collective-permute-start | bytes 884744 | tf_op jit(solution)/shard_map/ppermute | solution.py:18
  19.9 0.0 collective-permute-start.1
  19.9 2.1 %collective-permute-done.refs_1_ = bf16[192,768]{1,0:T(8,128)(2,1)S(1)} collective-permute-done((bf16[192,768]{1,0:T(8,128)(2,1)S(1)}, bf16[192,768]{1,0:T(8,128)(2,1)S(1)}, u32[]{:S(2)}, u32[]{:S(2)}) %collective-permute-start) | collective-permute-done | bytes 294944 | tf_op jit(solution)/shard_map/ppermute | solution.py:18
  22.0 5.9 %collective-permute-start.4 = (bf16[192,768]{1,0:T(8,128)(2,1)S(1)}, bf16[192,768]{1,0:T(8,128)(2,1)S(1)}, u32[]{:S(2)}, u32[]{:S(2)}) collective-permute-start(bf16[192,768]{1,0:T(8,128)(2,1)S(1)} %collective-permute-done.refs_1_), channel_id=1, source_target_pairs={{0,7},{1,0},{2,1},{3,2},{4,3},{5,4},{6,5},{7,6},{8,15},{9,8},{10,9... | collective-permute-start | bytes 884744 | tf_op jit(solution)/shard_map/ppermute | solution.py:18
  27.9 0.0 collective-permute-start.3
  27.9 0.0 collective-permute-done.2.refs_3_
  27.9 3.2 %collective-permute-start.6 = (bf16[192,768]{1,0:T(8,128)(2,1)S(1)}, bf16[192,768]{1,0:T(8,128)(2,1)S(1)}, u32[]{:S(2)}, u32[]{:S(2)}) collective-permute-start(bf16[192,768]{1,0:T(8,128)(2,1)S(1)} %collective-permute-done.2.refs_3_), channel_id=1, source_target_pairs={{0,7},{1,0},{2,1},{3,2},{4,3},{5,4},{6,5},{7,6},{8,15},{9,8},{10,9... | collective-permute-start | bytes 884744 | tf_op jit(solution)/shard_map/ppermute | solution.py:18
  31.1 0.0 collective-permute-done.1.refs_2_
  31.1 0.0 collective-permute-start.5
  31.1 4.2 %collective-permute-done.4.refs_5_ = bf16[192,768]{1,0:T(8,128)(2,1)S(1)} collective-permute-done((bf16[192,768]{1,0:T(8,128)(2,1)S(1)}, bf16[192,768]{1,0:T(8,128)(2,1)S(1)}, u32[]{:S(2)}, u32[]{:S(2)}) %collective-permute-start.4) | collective-permute-done | bytes 294944 | tf_op jit(solution)/shard_map/ppermute | solution.py:18
  35.3 3.7 %collective-permute-start.8 = (bf16[192,768]{1,0:T(8,128)(2,1)S(1)}, bf16[192,768]{1,0:T(8,128)(2,1)S(1)}, u32[]{:S(2)}, u32[]{:S(2)}) collective-permute-start(bf16[192,768]{1,0:T(8,128)(2,1)S(1)} %collective-permute-done.4.refs_5_), channel_id=1, source_target_pairs={{0,7},{1,0},{2,1},{3,2},{4,3},{5,4},{6,5},{7,6},{8,15},{9,8},{10,9... | collective-permute-start | bytes 884744 | tf_op jit(solution)/shard_map/ppermute | solution.py:18
  39.0 0.0 collective-permute-done.3.refs_4_
  39.0 0.0 collective-permute-start.7
  39.0 2.6 %collective-permute-done.6.refs_7_ = bf16[192,768]{1,0:T(8,128)(2,1)S(1)} collective-permute-done((bf16[192,768]{1,0:T(8,128)(2,1)S(1)}, bf16[192,768]{1,0:T(8,128)(2,1)S(1)}, u32[]{:S(2)}, u32[]{:S(2)}) %collective-permute-start.6) | collective-permute-done | bytes 294944 | tf_op jit(solution)/shard_map/ppermute | solution.py:18
  41.7 3.7 %collective-permute-start.10 = (bf16[192,768]{1,0:T(8,128)(2,1)S(1)}, bf16[192,768]{1,0:T(8,128)(2,1)S(1)}, u32[]{:S(2)}, u32[]{:S(2)}) collective-permute-start(bf16[192,768]{1,0:T(8,128)(2,1)S(1)} %collective-permute-done.6.refs_7_), channel_id=1, source_target_pairs={{0,7},{1,0},{2,1},{3,2},{4,3},{5,4},{6,5},{7,6},{8,15},{9,8},{10,9... | collective-permute-start | bytes 884744 | tf_op jit(solution)/shard_map/ppermute | solution.py:18
  45.4 0.0 collective-permute-done.5.refs_6_
  45.4 0.0 collective-permute-start.9
  45.4 2.6 %collective-permute-done.8.refs_1_ = bf16[192,768]{1,0:T(8,128)(2,1)S(1)} collective-permute-done((bf16[192,768]{1,0:T(8,128)(2,1)S(1)}, bf16[192,768]{1,0:T(8,128)(2,1)S(1)}, u32[]{:S(2)}, u32[]{:S(2)}) %collective-permute-start.8) | collective-permute-done | bytes 294944 | tf_op jit(solution)/shard_map/ppermute | solution.py:18
  48.0 3.7 %collective-permute-start.12 = (bf16[192,768]{1,0:T(8,128)(2,1)S(1)}, bf16[192,768]{1,0:T(8,128)(2,1)S(1)}, u32[]{:S(2)}, u32[]{:S(2)}) collective-permute-start(bf16[192,768]{1,0:T(8,128)(2,1)S(1)} %collective-permute-done.8.refs_1_), channel_id=1, source_target_pairs={{0,7},{1,0},{2,1},{3,2},{4,3},{5,4},{6,5},{7,6},{8,15},{9,8},{10,9... | collective-permute-start | bytes 884744 | tf_op jit(solution)/shard_map/ppermute | solution.py:18
  51.7 0.0 collective-permute-done.7.refs_0_
  51.7 0.0 collective-permute-start.11
  51.7 2.6 %collective-permute-done.10.refs_3_ = bf16[192,768]{1,0:T(8,128)(2,1)S(1)} collective-permute-done((bf16[192,768]{1,0:T(8,128)(2,1)S(1)}, bf16[192,768]{1,0:T(8,128)(2,1)S(1)}, u32[]{:S(2)}, u32[]{:S(2)}) %collective-permute-start.10) | collective-permute-done | bytes 294944 | tf_op jit(solution)/shard_map/ppermute | solution.py:18
  54.3 3.7 %collective-permute-done.9.refs_2_ = bf16[192,768]{1,0:T(8,128)(2,1)S(1)} collective-permute-done((bf16[192,768]{1,0:T(8,128)(2,1)S(1)}, bf16[192,768]{1,0:T(8,128)(2,1)S(1)}, u32[]{:S(2)}, u32[]{:S(2)}) %collective-permute-start.9) | collective-permute-done | bytes 294944 | tf_op jit(solution)/shard_map/ppermute | solution.py:18
  58.0 0.0 collective-permute-start.13
  58.0 0.6 collective-permute-done.12.refs_5_
  58.6 5.8 %collective-permute-done.11.refs_4_ = bf16[192,768]{1,0:T(8,128)(2,1)S(1)} collective-permute-done((bf16[192,768]{1,0:T(8,128)(2,1)S(1)}, bf16[192,768]{1,0:T(8,128)(2,1)S(1)}, u32[]{:S(2)}, u32[]{:S(2)}) %collective-permute-start.11) | collective-permute-done | bytes 294944 | tf_op jit(solution)/shard_map/ppermute | solution.py:18
  64.3 0.0 collective-permute-start.14
  64.3 1.1 %arrange_amplitudes.2.early_ref = bf16[768,1536]{1,0:T(8,128)(2,1)S(1)} custom-call(bf16[192,768]{1,0:T(8,128)(2,1)S(1)} %mask_amplitudes.1.refs_0_, bf16[192,768]{1,0:T(8,128)(2,1)S(1)} %collective-permute-done.refs_1_, bf16[192,768]{1,0:T(8,128)(2,1)S(1)} %collective-permute-done.1.refs_2_, bf16[192,768]{1,0:T(8,128)(2,1)S(1)} %collective-permute-done.2.refs_3_, ...), custom_call_target="tpu_custom_call" | custom-call | flops 100000000 | bytes 10000000 | tf_op jit(solution)/shard_map/arrange_amplitudes/pallas_call | solution.py:95
  65.4 0.0 copy-start.5
  65.4 0.0 copy-start.6
  65.4 2.9 %collective-permute-done.13.refs_6_ = bf16[192,768]{1,0:T(8,128)(2,1)S(1)} collective-permute-done((bf16[192,768]{1,0:T(8,128)(2,1)S(1)}, bf16[192,768]{1,0:T(8,128)(2,1)S(1)}, u32[]{:S(2)}, u32[]{:S(2)}) %collective-permute-start.13) | collective-permute-done | bytes 294944 | tf_op jit(solution)/shard_map/ppermute | solution.py:18
  68.3 2.8 %collective-permute-done.14.refs_7_ = bf16[192,768]{1,0:T(8,128)(2,1)S(1)} collective-permute-done((bf16[192,768]{1,0:T(8,128)(2,1)S(1)}, bf16[192,768]{1,0:T(8,128)(2,1)S(1)}, u32[]{:S(2)}, u32[]{:S(2)}) %collective-permute-start.14) | collective-permute-done | bytes 294944 | tf_op jit(solution)/shard_map/ppermute | solution.py:18
  71.0 1.1 %arrange_amplitudes.3.late_ref = bf16[768,1536]{1,0:T(8,128)(2,1)S(1)} custom-call(bf16[192,768]{1,0:T(8,128)(2,1)S(1)} %collective-permute-done.7.refs_0_, bf16[192,768]{1,0:T(8,128)(2,1)S(1)} %collective-permute-done.8.refs_1_, bf16[192,768]{1,0:T(8,128)(2,1)S(1)} %collective-permute-done.9.refs_2_, bf16[192,768]{1,0:T(8,128)(2,1)S(1)} %collective-permute-done.10.refs_3_, ...), custom_call_target="tpu_custom_call" | custom-call | flops 100000000 | bytes 10000000 | tf_op jit(solution)/shard_map/arrange_amplitudes/pallas_call | solution.py:95
  72.1 1.4 %copy-done.1 = bf16[768,1536]{1,0:T(8,128)(2,1)} copy-done((bf16[768,1536]{1,0:T(8,128)(2,1)}, bf16[768,1536]{1,0:T(8,128)(2,1)S(1)}, u32[]{:S(2)}) %copy-start.1) | copy-done | bytes 2359320
  73.5 0.0 copy-done.5
  73.5 15.5 %product.1 = bf16[768,1536]{1,0:T(8,128)(2,1)} custom-call(s32[8]{0:T(128)S(1)} %copy-done.5, s32[16]{0:T(128)S(1)} %copy-done.6, bf16[768,1536]{1,0:T(8,128)(2,1)S(1)} %arrange_amplitudes.2.early_ref, bf16[768,1536]{1,0:T(8,128)(2,1)} %copy-done.1, bf16[16,192,1536]{2,1,0:T(8,128)(2,1)} %bitcast.24, bf16[768,1536]{1,0:T(8,128)(2,1)} %prior_ref.1), custom_call_target="tpu_custom_call" | custom-call | flops 7247757312 | bytes 9437184 | tf_op jit(solution)/shard_map/product/pallas_call | solution.py:161
  (8 shorter events, 0.0 us)
Async XLA Ops:
  6.5 1.1 %copy-start = (bf16[16,12,1536]{2,0,1:T(8,128)(2,1)S(1)}, bf16[16,12,1536]{2,0,1:T(8,128)(2,1)}, u32[]{:S(2)}) copy-start(bf16[16,12,1536]{2,0,1:T(8,128)(2,1)} %param.7) | copy-start | bytes 1769476
  6.5 67.0 %all-gather.3.cloned.1.call-start = ((), (), s32[]{:S(2)}) async-start(), calls=%async_computation | async-start | bytes 10027008 | tf_op jit(solution)/shard_map/all_gather | solution.py:185
  8.8 1.0 %copy-start.2 = (bf16[768,192]{0,1:T(8,128)(2,1)S(1)}, bf16[768,192]{0,1:T(8,128)(2,1)}, u32[]{:S(2)}) copy-start(bf16[768,192]{0,1:T(8,128)(2,1)} %param.6) | copy-start | bytes 884740
  9.8 0.7 copy-start.3
  10.4 0.7 copy-start.4
  11.7 10.3 %collective-permute-start = (bf16[192,768]{1,0:T(8,128)(2,1)S(1)}, bf16[192,768]{1,0:T(8,128)(2,1)S(1)}, u32[]{:S(2)}, u32[]{:S(2)}) collective-permute-start(bf16[192,768]{1,0:T(8,128)(2,1)S(1)} %mask_amplitudes.1.refs_0_), channel_id=1, source_target_pairs={{0,8},{8,0},{1,9},{9,1},{2,10},{10,2},{3,11},{11,3},{4,12},{12,4},... | collective-permute-start | bytes 884744 | tf_op jit(solution)/shard_map/ppermute | solution.py:18
  14.1 13.8 %collective-permute-start.2 = (bf16[192,768]{1,0:T(8,128)(2,1)S(1)}, bf16[192,768]{1,0:T(8,128)(2,1)S(1)}, u32[]{:S(2)}, u32[]{:S(2)}) collective-permute-start(bf16[192,768]{1,0:T(8,128)(2,1)S(1)} %mask_amplitudes.1.refs_0_), channel_id=1, source_target_pairs={{0,7},{1,0},{2,1},{3,2},{4,3},{5,4},{6,5},{7,6},{8,15},{9,8},{10,9... | collective-permute-start | bytes 884744 | tf_op jit(solution)/shard_map/ppermute | solution.py:18
  19.9 11.2 %collective-permute-start.1 = (bf16[192,768]{1,0:T(8,128)(2,1)S(1)}, bf16[192,768]{1,0:T(8,128)(2,1)S(1)}, u32[]{:S(2)}, u32[]{:S(2)}) collective-permute-start(bf16[192,768]{1,0:T(8,128)(2,1)S(1)} %mask_amplitudes.1.refs_0_), channel_id=1, source_target_pairs={{0,1},{1,2},{2,3},{3,4},{4,5},{5,6},{6,7},{7,0},{8,9},{9,10},{10,1... | collective-permute-start | bytes 884744 | tf_op jit(solution)/shard_map/ppermute | solution.py:18
  22.0 13.3 %collective-permute-start.4 = (bf16[192,768]{1,0:T(8,128)(2,1)S(1)}, bf16[192,768]{1,0:T(8,128)(2,1)S(1)}, u32[]{:S(2)}, u32[]{:S(2)}) collective-permute-start(bf16[192,768]{1,0:T(8,128)(2,1)S(1)} %collective-permute-done.refs_1_), channel_id=1, source_target_pairs={{0,7},{1,0},{2,1},{3,2},{4,3},{5,4},{6,5},{7,6},{8,15},{9,8},{10,9... | collective-permute-start | bytes 884744 | tf_op jit(solution)/shard_map/ppermute | solution.py:18
  27.9 11.2 %collective-permute-start.3 = (bf16[192,768]{1,0:T(8,128)(2,1)S(1)}, bf16[192,768]{1,0:T(8,128)(2,1)S(1)}, u32[]{:S(2)}, u32[]{:S(2)}) collective-permute-start(bf16[192,768]{1,0:T(8,128)(2,1)S(1)} %collective-permute-done.refs_1_), channel_id=1, source_target_pairs={{0,1},{1,2},{2,3},{3,4},{4,5},{5,6},{6,7},{7,0},{8,9},{9,10},{10,1... | collective-permute-start | bytes 884744 | tf_op jit(solution)/shard_map/ppermute | solution.py:18
  27.9 13.8 %collective-permute-start.6 = (bf16[192,768]{1,0:T(8,128)(2,1)S(1)}, bf16[192,768]{1,0:T(8,128)(2,1)S(1)}, u32[]{:S(2)}, u32[]{:S(2)}) collective-permute-start(bf16[192,768]{1,0:T(8,128)(2,1)S(1)} %collective-permute-done.2.refs_3_), channel_id=1, source_target_pairs={{0,7},{1,0},{2,1},{3,2},{4,3},{5,4},{6,5},{7,6},{8,15},{9,8},{10,9... | collective-permute-start | bytes 884744 | tf_op jit(solution)/shard_map/ppermute | solution.py:18
  31.1 14.2 %collective-permute-start.5 = (bf16[192,768]{1,0:T(8,128)(2,1)S(1)}, bf16[192,768]{1,0:T(8,128)(2,1)S(1)}, u32[]{:S(2)}, u32[]{:S(2)}) collective-permute-start(bf16[192,768]{1,0:T(8,128)(2,1)S(1)} %collective-permute-done.1.refs_2_), channel_id=1, source_target_pairs={{0,1},{1,2},{2,3},{3,4},{4,5},{5,6},{6,7},{7,0},{8,9},{9,10},{10,1... | collective-permute-start | bytes 884744 | tf_op jit(solution)/shard_map/ppermute | solution.py:18
  35.3 12.6 %collective-permute-start.8 = (bf16[192,768]{1,0:T(8,128)(2,1)S(1)}, bf16[192,768]{1,0:T(8,128)(2,1)S(1)}, u32[]{:S(2)}, u32[]{:S(2)}) collective-permute-start(bf16[192,768]{1,0:T(8,128)(2,1)S(1)} %collective-permute-done.4.refs_5_), channel_id=1, source_target_pairs={{0,7},{1,0},{2,1},{3,2},{4,3},{5,4},{6,5},{7,6},{8,15},{9,8},{10,9... | collective-permute-start | bytes 884744 | tf_op jit(solution)/shard_map/ppermute | solution.py:18
  39.0 12.6 %collective-permute-start.7 = (bf16[192,768]{1,0:T(8,128)(2,1)S(1)}, bf16[192,768]{1,0:T(8,128)(2,1)S(1)}, u32[]{:S(2)}, u32[]{:S(2)}) collective-permute-start(bf16[192,768]{1,0:T(8,128)(2,1)S(1)} %collective-permute-done.3.refs_4_), channel_id=1, source_target_pairs={{0,1},{1,2},{2,3},{3,4},{4,5},{5,6},{6,7},{7,0},{8,9},{9,10},{10,1... | collective-permute-start | bytes 884744 | tf_op jit(solution)/shard_map/ppermute | solution.py:18
  41.7 12.6 %collective-permute-start.10 = (bf16[192,768]{1,0:T(8,128)(2,1)S(1)}, bf16[192,768]{1,0:T(8,128)(2,1)S(1)}, u32[]{:S(2)}, u32[]{:S(2)}) collective-permute-start(bf16[192,768]{1,0:T(8,128)(2,1)S(1)} %collective-permute-done.6.refs_7_), channel_id=1, source_target_pairs={{0,7},{1,0},{2,1},{3,2},{4,3},{5,4},{6,5},{7,6},{8,15},{9,8},{10,9... | collective-permute-start | bytes 884744 | tf_op jit(solution)/shard_map/ppermute | solution.py:18
  45.4 12.6 %collective-permute-start.9 = (bf16[192,768]{1,0:T(8,128)(2,1)S(1)}, bf16[192,768]{1,0:T(8,128)(2,1)S(1)}, u32[]{:S(2)}, u32[]{:S(2)}) collective-permute-start(bf16[192,768]{1,0:T(8,128)(2,1)S(1)} %collective-permute-done.5.refs_6_), channel_id=1, source_target_pairs={{0,1},{1,2},{2,3},{3,4},{4,5},{5,6},{6,7},{7,0},{8,9},{9,10},{10,1... | collective-permute-start | bytes 884744 | tf_op jit(solution)/shard_map/ppermute | solution.py:18
  48.0 10.6 %collective-permute-start.12 = (bf16[192,768]{1,0:T(8,128)(2,1)S(1)}, bf16[192,768]{1,0:T(8,128)(2,1)S(1)}, u32[]{:S(2)}, u32[]{:S(2)}) collective-permute-start(bf16[192,768]{1,0:T(8,128)(2,1)S(1)} %collective-permute-done.8.refs_1_), channel_id=1, source_target_pairs={{0,7},{1,0},{2,1},{3,2},{4,3},{5,4},{6,5},{7,6},{8,15},{9,8},{10,9... | collective-permute-start | bytes 884744 | tf_op jit(solution)/shard_map/ppermute | solution.py:18
  51.7 12.6 %collective-permute-start.11 = (bf16[192,768]{1,0:T(8,128)(2,1)S(1)}, bf16[192,768]{1,0:T(8,128)(2,1)S(1)}, u32[]{:S(2)}, u32[]{:S(2)}) collective-permute-start(bf16[192,768]{1,0:T(8,128)(2,1)S(1)} %collective-permute-done.7.refs_0_), channel_id=1, source_target_pairs={{0,1},{1,2},{2,3},{3,4},{4,5},{5,6},{6,7},{7,0},{8,9},{9,10},{10,1... | collective-permute-start | bytes 884744 | tf_op jit(solution)/shard_map/ppermute | solution.py:18
  58.0 10.3 %collective-permute-start.13 = (bf16[192,768]{1,0:T(8,128)(2,1)S(1)}, bf16[192,768]{1,0:T(8,128)(2,1)S(1)}, u32[]{:S(2)}, u32[]{:S(2)}) collective-permute-start(bf16[192,768]{1,0:T(8,128)(2,1)S(1)} %collective-permute-done.9.refs_2_), channel_id=1, source_target_pairs={{0,1},{1,2},{2,3},{3,4},{4,5},{5,6},{6,7},{7,0},{8,9},{9,10},{10,1... | collective-permute-start | bytes 884744 | tf_op jit(solution)/shard_map/ppermute | solution.py:18
  64.3 6.7 %collective-permute-start.14 = (bf16[192,768]{1,0:T(8,128)(2,1)S(1)}, bf16[192,768]{1,0:T(8,128)(2,1)S(1)}, u32[]{:S(2)}, u32[]{:S(2)}) collective-permute-start(bf16[192,768]{1,0:T(8,128)(2,1)S(1)} %collective-permute-done.12.refs_5_), channel_id=1, source_target_pairs={{0,7},{1,0},{2,1},{3,2},{4,3},{5,4},{6,5},{7,6},{8,15},{9,8},{10,9... | collective-permute-start | bytes 884744 | tf_op jit(solution)/shard_map/ppermute | solution.py:18
  65.4 8.1 %copy-start.5 = (s32[8]{0:T(128)S(1)}, s32[8]{0:T(128)}, u32[]{:S(2)}) copy-start(s32[8]{0:T(128)} %pair_ref.3) | copy-start | bytes 100
  65.4 8.1 %copy-start.6 = (s32[16]{0:T(128)S(1)}, s32[16]{0:T(128)}, u32[]{:S(2)}) copy-start(s32[16]{0:T(128)} %ab_ref.1) | copy-start | bytes 196
  72.1 1.4 %copy-start.1 = (bf16[768,1536]{1,0:T(8,128)(2,1)}, bf16[768,1536]{1,0:T(8,128)(2,1)S(1)}, u32[]{:S(2)}) copy-start(bf16[768,1536]{1,0:T(8,128)(2,1)S(1)} %arrange_amplitudes.3.late_ref) | copy-start | bytes 7077892
Sparse Core Ops, SparseCore 0:
  9.2 62.1 all-gather.2

commit v3 on v2

--- a/solution.py
+++ b/solution.py
@@ -38,31 +38,6 @@
     return found
 
 
-def mask_kernel(pair_ref, cd_ref, amp_ref, out_ref):
-    group = lax.axis_index("yhi") * lax.axis_size("z") + lax.axis_index("z")
-    column = lax.broadcasted_iota(jnp.int32, (1, amp_ref.shape[1]), 1)
-    labels = jnp.full(column.shape, pair_ref[0])
-    for tile in range(1, pair_ref.shape[0]):
-        labels = jnp.where(column >= tile * TILE, pair_ref[tile], labels)
-    for tile in range(amp_ref.shape[0] // TILE):
-        rows = slice(tile * TILE, (tile + 1) * TILE)
-        kept = labels == cd_ref[group * 2 + tile]
-        out_ref[rows] = jnp.where(kept, amp_ref[rows].astype(jnp.float32), 0.0).astype(out_ref.dtype)
-
-
-def masked(amplitudes, pair_class, cd_class):
-    smem = pl.BlockSpec(memory_space=pltpu.SMEM)
-    vmem = pl.BlockSpec(memory_space=pltpu.VMEM)
-    return pl.pallas_call(
-        mask_kernel,
-        out_shape=jax.ShapeDtypeStruct(amplitudes.shape, amplitudes.dtype),
-        in_specs=[smem, smem, vmem],
-        out_specs=vmem,
-        compiler_params=pltpu.CompilerParams(vmem_limit_bytes=24 << 20),
-        name="mask_amplitudes",
-    )(pair_class, cd_class, amplitudes)
-
-
 def ordered(integrals, order):
     groups, part, width = integrals.shape
     flat = integrals.transpose(1, 0, 2).reshape(part * groups, width)
@@ -71,36 +46,52 @@
     return jnp.dot(chosen.astype(integrals.dtype), flat, preferred_element_type=jnp.float32).astype(integrals.dtype)
 
 
-def arrange(chunk_refs, out_ref):
+def group_of(plane, step):
+    count = lax.axis_size("z")
+    return lax.rem(lax.axis_index("yhi") + plane, 2) * count + lax.rem(lax.axis_index("z") + step + count, count)
+
+
+def arrange_kernel(places, pair_ref, cd_ref, *refs):
+    *chunk_refs, out_ref = refs
     wide, part = 128, 12
+    size = out_ref.shape[1] // 4
+    steps = out_ref.shape[0] // wide
+    classes = [[cd_ref[2 * group_of(*place) + tile] for tile in (0, 1)] for place in places]
 
-    @pl.loop(0, out_ref.shape[0] // wide)
+    @pl.loop(0, steps)
     def _(step):
         lanes = pl.ds(pl.multiple_of(step * wide, wide), wide)
-        size = out_ref.shape[1] // 4
+        column = step * wide + lax.broadcasted_iota(jnp.int32, (1, wide), 1)
+        labels = jnp.full(column.shape, pair_ref[0])
+        for tile in range(1, pair_ref.shape[0]):
+            labels = jnp.where(column >= tile * TILE, pair_ref[tile], labels)
         for quad in range(4):
+            keep = [labels == both[quad // 2] for both in classes]
             pieces = [[], [], [], []]
             for pair in (0, 2):
                 at = (quad * 4 + pair) * part
-                for chunk in chunk_refs:
-                    both = chunk[at : at + 2 * part, lanes].astype(jnp.float32)
+                for chunk, kept in zip(chunk_refs, keep):
+                    both = jnp.where(kept, chunk[at : at + 2 * part, lanes].astype(jnp.float32), 0.0)
                     pieces[pair].append(both[:part])
                     pieces[pair + 1].append(both[part:])
             block = jnp.concatenate(sum(pieces, []))
             out_ref[lanes, quad * size : (quad + 1) * size] = block.T.astype(out_ref.dtype)
 
 
-def arranged(chunks):
+def arranged(found, pair_class, cd_class):
+    chunks = [chunk for chunk, _, _ in found]
     deep, wide = chunks[0].shape
+    shape = (wide, len(chunks) * deep)
+    smem, vmem = (pl.BlockSpec(memory_space=space) for space in (pltpu.SMEM, pltpu.VMEM))
     return pl.pallas_call(
-        lambda *refs: arrange(refs[:-1], refs[-1]),
-        out_shape=jax.ShapeDtypeStruct((wide, len(chunks) * deep), chunks[0].dtype),
-        in_specs=[pl.BlockSpec(memory_space=pltpu.VMEM)] * len(chunks),
-        out_specs=pl.BlockSpec(memory_space=pltpu.VMEM),
+        functools.partial(arrange_kernel, [place for _, *place in found]),
+        out_shape=jax.ShapeDtypeStruct(shape, chunks[0].dtype),
+        in_specs=[smem, smem] + [vmem] * len(chunks),
+        out_specs=vmem,
         compiler_params=pltpu.CompilerParams(vmem_limit_bytes=24 << 20),
         cost_estimate=pl.CostEstimate(flops=10**8, bytes_accessed=10**7, transcendentals=0),
         name="arrange_amplitudes",
-    )(*chunks)
+    )(pair_class, cd_class, *chunks)
 
 
 def product_kernel(block, pair_ref, ab_ref, early_ref, late_ref, panel_ref, prior_ref, out_ref, late, held, prior, done, late_sem, sems):
@@ -120,31 +111,38 @@
     def fetch_prior(step):
         return pltpu.make_async_copy(prior_ref.at[:, columns(step)], prior.at[:, columns(step)], prior_sem.at[step])
 
-    fetch_late = pltpu.make_async_copy(late_ref, late, late_sem)
-    fetch_late.start()
-    for step in range(steps):
-        fetch(step).start()
-        fetch_prior(step).start()
-    fetch_late.wait()
+    def times(amp, at, lanes):
+        panel = held[:, at : at + half, lanes].reshape(deep, block)
+        return jnp.dot(amp[...], panel, preferred_element_type=jnp.float32)
 
-    @pl.loop(0, steps)
-    def _(step):
-        fetch(step).wait()
+    def finish(step, ladder):
         lanes = columns(step)
         column = step * block + lax.broadcasted_iota(jnp.int32, (1, block), 1)
         labels = jnp.full((1, block), ab_ref[0])
         for tile in range(1, ab_ref.shape[0]):
             labels = jnp.where(column >= tile * TILE, ab_ref[tile], labels)
-        ladder = sum(
-            jnp.dot(amp[...], held[:, at : at + half, lanes].reshape(deep, block), preferred_element_type=jnp.float32)
-            for amp, at in ((early_ref, 0), (late, half))
-        )
         fetch_prior(step).wait()
         for tile in range(out_ref.shape[0] // TILE):
             rows = slice(tile * TILE, (tile + 1) * TILE)
             kept = jnp.where(labels == pair_ref[tile], ladder[rows], 0.0)
             done[rows, lanes] = (prior[rows, lanes].astype(jnp.float32) + kept).astype(done.dtype)
         put(step).start()
+
+    fetch_late = pltpu.make_async_copy(late_ref, late, late_sem)
+    fetch(0).start()
+    fetch_late.start()
+    fetch_prior(0).start()
+    fetch(0).wait()
+    fetch_late.wait()
+    for step in range(1, steps):
+        fetch(step).start()
+        fetch_prior(step).start()
+    finish(0, times(early_ref, 0, pl.ds(0, block)) + times(late, half, pl.ds(0, block)))
+
+    @pl.loop(1, steps)
+    def _(step):
+        fetch(step).wait()
+        finish(step, times(early_ref, 0, columns(step)) + times(late, half, columns(step)))
 
     for step in range(steps):
         put(step).wait()
@@ -178,14 +176,13 @@
 
 
 def local(amplitudes, integrals, residual_in, pair_class, cd_class, ab_class):
-    count = lax.axis_size("z")
-    z, side = lax.axis_index("z"), lax.axis_index("yhi")
-    found = ring(masked(amplitudes.T, pair_class, cd_class))
-    order = jnp.stack([(side ^ plane) * count + (z + step) % count for _, plane, step in found])
+    found = ring(amplitudes.T)
+    order = jnp.stack([group_of(*place) for _, *place in found])
     panel = lax.all_gather(ordered(integrals, order), ROW, axis=0)
     half = len(found) // 2
-    chunks = [chunk for chunk, _, _ in found]
-    return finished(arranged(chunks[:half]), arranged(chunks[half:]), panel, residual_in, pair_class, ab_class)
+    early = arranged(found[:half], pair_class, cd_class)
+    late = arranged(found[half:], pair_class, cd_class)
+    return finished(early, late, panel, residual_in, pair_class, ab_class)
 
 
 def solution(mesh):

time: 96.1 us -> 92.7 us (0.965); the launches traced: 95.9 us -> 90.9 us
  waiting for transfers between devices: 29.8 us -> 27.1 us
  Pallas kernels: 18.3 us -> 16 us
    pallas_call x1, Pallas kernels: 15.5 us -> 12.6 us  [finished(): pl.pallas_call(functools.partial(product_kernel, block), out_shape=jax.Sh...]
    ppermute x15, waiting for transfers between devices: 29.8 us -> 27.1 us  [shift(): lax.ppermute(value, axis, [(i, (i + steps) % count) for i in range(count)])]
    pallas_call x3 -> x2, Pallas kernels: 2.74 us -> 3.45 us  [arranged(): pl.pallas_call(functools.partial(arrange_kernel, [place for _, *place in...]
  transfers between devices with their start and end apart: 16 -> 16, of which waited for: 10 -> 9; matrix products, arithmetic and copies ran while one was open for 0% -> 0% of each run, Pallas kernels for 3% -> 4%
where the time goes in v3:
time: 92.7 us; the launch traced here: 90.9 us
  starting transfers between devices  28.4 us (31%)
  waiting for transfers between devices  27.1 us (29%)
  Pallas kernels  16 us (17%)
  between operations  13.5 us (15%)
  local copies, waits for them, and re-layouts  4.65 us (5%)
  matrix products  1.17 us (1%)
    ppermute x15, starting transfers between devices, shift(): lax.ppermute(value, axis, [(i, (i + steps) % count) for i in range(count)])  28.4 us
    ppermute x15, waiting for transfers between devices, shift(): lax.ppermute(value, axis, [(i, (i + steps) % count) for i in range(count)])  27.1 us
    pallas_call x1, Pallas kernels, finished(): pl.pallas_call(functools.partial(product_kernel, block), out_shape=jax.Sh...  12.6 us
    unnamed x14, local copies, waits for them, and re-layouts  4.47 us
    pallas_call x2, Pallas kernels, arranged(): pl.pallas_call(functools.partial(arrange_kernel, [place for _, *place in...  3.45 us
  transfers between devices with their start and end apart: 16, of which 9 were waited for; matrix products, arithmetic and copies ran while one was open for 0% of the time, Pallas kernels for 4%

profile of v3, /device:TPU:12, one launch (start us, length us, event | category | flops | bytes accessed | tf_op | source)
XLA Modules:
  0.0 90.9 jit_solution(18362414885011583522)
XLA Ops:
  6.5 0.0 copy-start
  6.5 0.0 all-gather.3.cloned.1.call-start
  6.5 0.1 stack.67
  6.6 0.1 broadcast_add_fusion
  6.7 0.1 add.166
  6.8 0.8 copy-done
  7.6 1.2 %convolution_convert_fusion = bf16[192,1536]{1,0:T(8,128)(2,1)} fusion(bf16[192,1536]{1,0:T(8,128)(2,1)S(1)} %bitcast.22, s32[192]{0:T(256)S(1)} %add.166), kind=kOutput, calls=%fused_computation | convolution fusion | flops 113577984 | bytes 1180416 | tf_op jit(solution)/shard_map/dot_general | solution.py:46
  8.8 0.0 all-gather.3.cloned.1.call-update
  8.8 2.4 %collective-permute-start = (bf16[192,768]{1,0:T(8,128)(2,1)}, bf16[192,768]{1,0:T(8,128)(2,1)S(1)}, u32[]{:S(2)}, u32[]{:S(2)}) collective-permute-start(bf16[192,768]{1,0:T(8,128)(2,1)} %bitcast.23), channel_id=1, source_target_pairs={{0,8},{8,0},{1,9},{9,1},{2,10},{10,2},{3,11},{11,3},{4,12},{12,4},... | collective-permute-start | bytes 884744 | tf_op jit(solution)/shard_map/ppermute | solution.py:18
  11.2 5.9 %collective-permute-start.2 = (bf16[192,768]{1,0:T(8,128)(2,1)}, bf16[192,768]{1,0:T(8,128)(2,1)S(1)}, u32[]{:S(2)}, u32[]{:S(2)}) collective-permute-start(bf16[192,768]{1,0:T(8,128)(2,1)} %bitcast.24), channel_id=1, source_target_pairs={{0,7},{1,0},{2,1},{3,2},{4,3},{5,4},{6,5},{7,6},{8,15},{9,8},{10,9... | collective-permute-start | bytes 884744 | tf_op jit(solution)/shard_map/ppermute | solution.py:18
  17.0 0.0 collective-permute-start.1
  17.0 2.3 %collective-permute-done.refs_1_ = bf16[192,768]{1,0:T(8,128)(2,1)S(1)} collective-permute-done((bf16[192,768]{1,0:T(8,128)(2,1)}, bf16[192,768]{1,0:T(8,128)(2,1)S(1)}, u32[]{:S(2)}, u32[]{:S(2)}) %collective-permute-start) | collective-permute-done | bytes 294944 | tf_op jit(solution)/shard_map/ppermute | solution.py:18
  19.4 5.9 %collective-permute-start.4 = (bf16[192,768]{1,0:T(8,128)(2,1)S(1)}, bf16[192,768]{1,0:T(8,128)(2,1)S(1)}, u32[]{:S(2)}, u32[]{:S(2)}) collective-permute-start(bf16[192,768]{1,0:T(8,128)(2,1)S(1)} %collective-permute-done.refs_1_), channel_id=1, source_target_pairs={{0,7},{1,0},{2,1},{3,2},{4,3},{5,4},{6,5},{7,6},{8,15},{9,8},{10,9... | collective-permute-start | bytes 884744 | tf_op jit(solution)/shard_map/ppermute | solution.py:18
  25.2 0.0 collective-permute-start.3
  25.2 0.0 collective-permute-done.2.refs_3_
  25.2 3.2 %collective-permute-start.6 = (bf16[192,768]{1,0:T(8,128)(2,1)S(1)}, bf16[192,768]{1,0:T(8,128)(2,1)S(1)}, u32[]{:S(2)}, u32[]{:S(2)}) collective-permute-start(bf16[192,768]{1,0:T(8,128)(2,1)S(1)} %collective-permute-done.2.refs_3_), channel_id=1, source_target_pairs={{0,7},{1,0},{2,1},{3,2},{4,3},{5,4},{6,5},{7,6},{8,15},{9,8},{10,9... | collective-permute-start | bytes 884744 | tf_op jit(solution)/shard_map/ppermute | solution.py:18
  28.4 0.0 collective-permute-done.1.refs_2_
  28.4 0.0 collective-permute-start.5
  28.5 4.2 %collective-permute-done.4.refs_5_ = bf16[192,768]{1,0:T(8,128)(2,1)S(1)} collective-permute-done((bf16[192,768]{1,0:T(8,128)(2,1)S(1)}, bf16[192,768]{1,0:T(8,128)(2,1)S(1)}, u32[]{:S(2)}, u32[]{:S(2)}) %collective-permute-start.4) | collective-permute-done | bytes 294944 | tf_op jit(solution)/shard_map/ppermute | solution.py:18
  32.7 3.7 %collective-permute-start.8 = (bf16[192,768]{1,0:T(8,128)(2,1)S(1)}, bf16[192,768]{1,0:T(8,128)(2,1)S(1)}, u32[]{:S(2)}, u32[]{:S(2)}) collective-permute-start(bf16[192,768]{1,0:T(8,128)(2,1)S(1)} %collective-permute-done.4.refs_5_), channel_id=1, source_target_pairs={{0,7},{1,0},{2,1},{3,2},{4,3},{5,4},{6,5},{7,6},{8,15},{9,8},{10,9... | collective-permute-start | bytes 884744 | tf_op jit(solution)/shard_map/ppermute | solution.py:18
  36.4 0.0 collective-permute-done.3.refs_4_
  36.4 0.0 collective-permute-start.7
  36.4 2.6 %collective-permute-done.6.refs_7_ = bf16[192,768]{1,0:T(8,128)(2,1)S(1)} collective-permute-done((bf16[192,768]{1,0:T(8,128)(2,1)S(1)}, bf16[192,768]{1,0:T(8,128)(2,1)S(1)}, u32[]{:S(2)}, u32[]{:S(2)}) %collective-permute-start.6) | collective-permute-done | bytes 294944 | tf_op jit(solution)/shard_map/ppermute | solution.py:18
  39.0 3.7 %collective-permute-start.10 = (bf16[192,768]{1,0:T(8,128)(2,1)S(1)}, bf16[192,768]{1,0:T(8,128)(2,1)S(1)}, u32[]{:S(2)}, u32[]{:S(2)}) collective-permute-start(bf16[192,768]{1,0:T(8,128)(2,1)S(1)} %collective-permute-done.6.refs_7_), channel_id=1, source_target_pairs={{0,7},{1,0},{2,1},{3,2},{4,3},{5,4},{6,5},{7,6},{8,15},{9,8},{10,9... | collective-permute-start | bytes 884744 | tf_op jit(solution)/shard_map/ppermute | solution.py:18
  42.7 0.0 collective-permute-done.5.refs_6_
  42.7 0.0 collective-permute-start.9
  42.7 2.6 %collective-permute-done.8.refs_1_ = bf16[192,768]{1,0:T(8,128)(2,1)S(1)} collective-permute-done((bf16[192,768]{1,0:T(8,128)(2,1)S(1)}, bf16[192,768]{1,0:T(8,128)(2,1)S(1)}, u32[]{:S(2)}, u32[]{:S(2)}) %collective-permute-start.8) | collective-permute-done | bytes 294944 | tf_op jit(solution)/shard_map/ppermute | solution.py:18
  45.3 3.7 %collective-permute-start.12 = (bf16[192,768]{1,0:T(8,128)(2,1)S(1)}, bf16[192,768]{1,0:T(8,128)(2,1)S(1)}, u32[]{:S(2)}, u32[]{:S(2)}) collective-permute-start(bf16[192,768]{1,0:T(8,128)(2,1)S(1)} %collective-permute-done.8.refs_1_), channel_id=1, source_target_pairs={{0,7},{1,0},{2,1},{3,2},{4,3},{5,4},{6,5},{7,6},{8,15},{9,8},{10,9... | collective-permute-start | bytes 884744 | tf_op jit(solution)/shard_map/ppermute | solution.py:18
  49.0 0.0 collective-permute-done.7.refs_0_
  49.0 0.0 collective-permute-start.11
  49.0 2.6 %collective-permute-done.10.refs_3_ = bf16[192,768]{1,0:T(8,128)(2,1)S(1)} collective-permute-done((bf16[192,768]{1,0:T(8,128)(2,1)S(1)}, bf16[192,768]{1,0:T(8,128)(2,1)S(1)}, u32[]{:S(2)}, u32[]{:S(2)}) %collective-permute-start.10) | collective-permute-done | bytes 294944 | tf_op jit(solution)/shard_map/ppermute | solution.py:18
  51.6 3.7 %collective-permute-done.9.refs_2_ = bf16[192,768]{1,0:T(8,128)(2,1)S(1)} collective-permute-done((bf16[192,768]{1,0:T(8,128)(2,1)S(1)}, bf16[192,768]{1,0:T(8,128)(2,1)S(1)}, u32[]{:S(2)}, u32[]{:S(2)}) %collective-permute-start.9) | collective-permute-done | bytes 294944 | tf_op jit(solution)/shard_map/ppermute | solution.py:18
  55.3 0.0 collective-permute-start.13
  55.3 0.6 collective-permute-done.12.refs_5_
  55.9 5.8 %collective-permute-done.11.refs_4_ = bf16[192,768]{1,0:T(8,128)(2,1)S(1)} collective-permute-done((bf16[192,768]{1,0:T(8,128)(2,1)S(1)}, bf16[192,768]{1,0:T(8,128)(2,1)S(1)}, u32[]{:S(2)}, u32[]{:S(2)}) %collective-permute-start.11) | collective-permute-done | bytes 294944 | tf_op jit(solution)/shard_map/ppermute | solution.py:18
  61.6 0.0 collective-permute-start.14
  61.6 1.0 %copy-done.2 = bf16[768,192]{0,1:T(8,128)(2,1)S(1)} copy-done((bf16[768,192]{0,1:T(8,128)(2,1)S(1)}, bf16[768,192]{0,1:T(8,128)(2,1)}, u32[]{:S(2)}) %copy-start.2) | copy-done | bytes 294936
  62.6 0.7 copy-done.3
  63.3 0.7 copy-done.4
  63.9 1.7 %arrange_amplitudes.2.early_ref = bf16[768,1536]{1,0:T(8,128)(2,1)S(1)} custom-call(s32[8]{0:T(128)S(1)} %copy-done.4, s32[32]{0:T(128)S(1)} %copy-done.3, bf16[192,768]{1,0:T(8,128)(2,1)S(1)} %bitcast.26, bf16[192,768]{1,0:T(8,128)(2,1)S(1)} %collective-permute-done.refs_1_, bf16[192,768]{1,0:T(8,128)(2,1)S(1)} %collective-permute-done.1.refs_2_, ...), custom_call_target="tpu_custom_call" | custom-call | flops 100000000 | bytes 10000000 | tf_op jit(solution)/shard_map/arrange_amplitudes/pallas_call | solution.py:86
  65.6 0.0 copy-start.5
  65.7 0.0 copy-start.6
  65.7 0.0 collective-permute-done.13.refs_6_
  65.7 2.7 %collective-permute-done.14.refs_7_ = bf16[192,768]{1,0:T(8,128)(2,1)S(1)} collective-permute-done((bf16[192,768]{1,0:T(8,128)(2,1)S(1)}, bf16[192,768]{1,0:T(8,128)(2,1)S(1)}, u32[]{:S(2)}, u32[]{:S(2)}) %collective-permute-start.14) | collective-permute-done | bytes 294944 | tf_op jit(solution)/shard_map/ppermute | solution.py:18
  68.4 1.7 %arrange_amplitudes.3.late_ref = bf16[768,1536]{1,0:T(8,128)(2,1)S(1)} custom-call(s32[8]{0:T(128)S(1)} %copy-done.4, s32[32]{0:T(128)S(1)} %copy-done.3, bf16[192,768]{1,0:T(8,128)(2,1)S(1)} %collective-permute-done.7.refs_0_, bf16[192,768]{1,0:T(8,128)(2,1)S(1)} %collective-permute-done.8.refs_1_, bf16[192,768]{1,0:T(8,128)(2,1)S(1)} %collective-permute-done.9.refs_2_, ...), custom_call_target="tpu_custom_call" | custom-call | flops 100000000 | bytes 10000000 | tf_op jit(solution)/shard_map/arrange_amplitudes/pallas_call | solution.py:86
  70.1 0.0 copy-start.1
  70.1 1.4 %copy-done.1 = bf16[768,1536]{1,0:T(8,128)(2,1)} copy-done((bf16[768,1536]{1,0:T(8,128)(2,1)}, bf16[768,1536]{1,0:T(8,128)(2,1)S(1)}, u32[]{:S(2)}) %copy-start.1) | copy-done | bytes 2359320
  71.5 12.6 %product.1 = bf16[768,1536]{1,0:T(8,128)(2,1)} custom-call(s32[8]{0:T(128)S(1)} %copy-done.5, s32[16]{0:T(128)S(1)} %copy-done.6, bf16[768,1536]{1,0:T(8,128)(2,1)S(1)} %arrange_amplitudes.2.early_ref, bf16[768,1536]{1,0:T(8,128)(2,1)} %copy-done.1, bf16[16,192,1536]{2,1,0:T(8,128)(2,1)} %bitcast.27, bf16[768,1536]{1,0:T(8,128)(2,1)} %prior_ref.1), custom_call_target="tpu_custom_call" | custom-call | flops 7247757312 | bytes 9437184 | tf_op jit(solution)/shard_map/product/pallas_call | solution.py:159
  (7 shorter events, 0.0 us)
Async XLA Ops:
  6.5 1.1 %copy-start = (bf16[16,12,1536]{2,0,1:T(8,128)(2,1)S(1)}, bf16[16,12,1536]{2,0,1:T(8,128)(2,1)}, u32[]{:S(2)}) copy-start(bf16[16,12,1536]{2,0,1:T(8,128)(2,1)} %param.7) | copy-start | bytes 1769476
  6.5 65.0 %all-gather.3.cloned.1.call-start = ((), (), s32[]{:S(2)}) async-start(), calls=%async_computation | async-start | bytes 10027008 | tf_op jit(solution)/shard_map/all_gather | solution.py:181
  8.8 10.6 %collective-permute-start = (bf16[192,768]{1,0:T(8,128)(2,1)}, bf16[192,768]{1,0:T(8,128)(2,1)S(1)}, u32[]{:S(2)}, u32[]{:S(2)}) collective-permute-start(bf16[192,768]{1,0:T(8,128)(2,1)} %bitcast.23), channel_id=1, source_target_pairs={{0,8},{8,0},{1,9},{9,1},{2,10},{10,2},{3,11},{11,3},{4,12},{12,4},... | collective-permute-start | bytes 884744 | tf_op jit(solution)/shard_map/ppermute | solution.py:18
  11.2 14.0 %collective-permute-start.2 = (bf16[192,768]{1,0:T(8,128)(2,1)}, bf16[192,768]{1,0:T(8,128)(2,1)S(1)}, u32[]{:S(2)}, u32[]{:S(2)}) collective-permute-start(bf16[192,768]{1,0:T(8,128)(2,1)} %bitcast.24), channel_id=1, source_target_pairs={{0,7},{1,0},{2,1},{3,2},{4,3},{5,4},{6,5},{7,6},{8,15},{9,8},{10,9... | collective-permute-start | bytes 884744 | tf_op jit(solution)/shard_map/ppermute | solution.py:18
  17.0 11.4 %collective-permute-start.1 = (bf16[192,768]{1,0:T(8,128)(2,1)}, bf16[192,768]{1,0:T(8,128)(2,1)S(1)}, u32[]{:S(2)}, u32[]{:S(2)}) collective-permute-start(bf16[192,768]{1,0:T(8,128)(2,1)} %bitcast.25), channel_id=1, source_target_pairs={{0,1},{1,2},{2,3},{3,4},{4,5},{5,6},{6,7},{7,0},{8,9},{9,10},{10,1... | collective-permute-start | bytes 884744 | tf_op jit(solution)/shard_map/ppermute | solution.py:18
  19.4 13.3 %collective-permute-start.4 = (bf16[192,768]{1,0:T(8,128)(2,1)S(1)}, bf16[192,768]{1,0:T(8,128)(2,1)S(1)}, u32[]{:S(2)}, u32[]{:S(2)}) collective-permute-start(bf16[192,768]{1,0:T(8,128)(2,1)S(1)} %collective-permute-done.refs_1_), channel_id=1, source_target_pairs={{0,7},{1,0},{2,1},{3,2},{4,3},{5,4},{6,5},{7,6},{8,15},{9,8},{10,9... | collective-permute-start | bytes 884744 | tf_op jit(solution)/shard_map/ppermute | solution.py:18
  25.2 11.2 %collective-permute-start.3 = (bf16[192,768]{1,0:T(8,128)(2,1)S(1)}, bf16[192,768]{1,0:T(8,128)(2,1)S(1)}, u32[]{:S(2)}, u32[]{:S(2)}) collective-permute-start(bf16[192,768]{1,0:T(8,128)(2,1)S(1)} %collective-permute-done.refs_1_), channel_id=1, source_target_pairs={{0,1},{1,2},{2,3},{3,4},{4,5},{5,6},{6,7},{7,0},{8,9},{9,10},{10,1... | collective-permute-start | bytes 884744 | tf_op jit(solution)/shard_map/ppermute | solution.py:18
  25.2 13.8 %collective-permute-start.6 = (bf16[192,768]{1,0:T(8,128)(2,1)S(1)}, bf16[192,768]{1,0:T(8,128)(2,1)S(1)}, u32[]{:S(2)}, u32[]{:S(2)}) collective-permute-start(bf16[192,768]{1,0:T(8,128)(2,1)S(1)} %collective-permute-done.2.refs_3_), channel_id=1, source_target_pairs={{0,7},{1,0},{2,1},{3,2},{4,3},{5,4},{6,5},{7,6},{8,15},{9,8},{10,9... | collective-permute-start | bytes 884744 | tf_op jit(solution)/shard_map/ppermute | solution.py:18
  28.4 14.2 %collective-permute-start.5 = (bf16[192,768]{1,0:T(8,128)(2,1)S(1)}, bf16[192,768]{1,0:T(8,128)(2,1)S(1)}, u32[]{:S(2)}, u32[]{:S(2)}) collective-permute-start(bf16[192,768]{1,0:T(8,128)(2,1)S(1)} %collective-permute-done.1.refs_2_), channel_id=1, source_target_pairs={{0,1},{1,2},{2,3},{3,4},{4,5},{5,6},{6,7},{7,0},{8,9},{9,10},{10,1... | collective-permute-start | bytes 884744 | tf_op jit(solution)/shard_map/ppermute | solution.py:18
  32.7 12.6 %collective-permute-start.8 = (bf16[192,768]{1,0:T(8,128)(2,1)S(1)}, bf16[192,768]{1,0:T(8,128)(2,1)S(1)}, u32[]{:S(2)}, u32[]{:S(2)}) collective-permute-start(bf16[192,768]{1,0:T(8,128)(2,1)S(1)} %collective-permute-done.4.refs_5_), channel_id=1, source_target_pairs={{0,7},{1,0},{2,1},{3,2},{4,3},{5,4},{6,5},{7,6},{8,15},{9,8},{10,9... | collective-permute-start | bytes 884744 | tf_op jit(solution)/shard_map/ppermute | solution.py:18
  36.4 12.6 %collective-permute-start.7 = (bf16[192,768]{1,0:T(8,128)(2,1)S(1)}, bf16[192,768]{1,0:T(8,128)(2,1)S(1)}, u32[]{:S(2)}, u32[]{:S(2)}) collective-permute-start(bf16[192,768]{1,0:T(8,128)(2,1)S(1)} %collective-permute-done.3.refs_4_), channel_id=1, source_target_pairs={{0,1},{1,2},{2,3},{3,4},{4,5},{5,6},{6,7},{7,0},{8,9},{9,10},{10,1... | collective-permute-start | bytes 884744 | tf_op jit(solution)/shard_map/ppermute | solution.py:18
  39.0 12.6 %collective-permute-start.10 = (bf16[192,768]{1,0:T(8,128)(2,1)S(1)}, bf16[192,768]{1,0:T(8,128)(2,1)S(1)}, u32[]{:S(2)}, u32[]{:S(2)}) collective-permute-start(bf16[192,768]{1,0:T(8,128)(2,1)S(1)} %collective-permute-done.6.refs_7_), channel_id=1, source_target_pairs={{0,7},{1,0},{2,1},{3,2},{4,3},{5,4},{6,5},{7,6},{8,15},{9,8},{10,9... | collective-permute-start | bytes 884744 | tf_op jit(solution)/shard_map/ppermute | solution.py:18
  42.7 12.6 %collective-permute-start.9 = (bf16[192,768]{1,0:T(8,128)(2,1)S(1)}, bf16[192,768]{1,0:T(8,128)(2,1)S(1)}, u32[]{:S(2)}, u32[]{:S(2)}) collective-permute-start(bf16[192,768]{1,0:T(8,128)(2,1)S(1)} %collective-permute-done.5.refs_6_), channel_id=1, source_target_pairs={{0,1},{1,2},{2,3},{3,4},{4,5},{5,6},{6,7},{7,0},{8,9},{9,10},{10,1... | collective-permute-start | bytes 884744 | tf_op jit(solution)/shard_map/ppermute | solution.py:18
  45.3 10.6 %collective-permute-start.12 = (bf16[192,768]{1,0:T(8,128)(2,1)S(1)}, bf16[192,768]{1,0:T(8,128)(2,1)S(1)}, u32[]{:S(2)}, u32[]{:S(2)}) collective-permute-start(bf16[192,768]{1,0:T(8,128)(2,1)S(1)} %collective-permute-done.8.refs_1_), channel_id=1, source_target_pairs={{0,7},{1,0},{2,1},{3,2},{4,3},{5,4},{6,5},{7,6},{8,15},{9,8},{10,9... | collective-permute-start | bytes 884744 | tf_op jit(solution)/shard_map/ppermute | solution.py:18
  49.0 12.6 %collective-permute-start.11 = (bf16[192,768]{1,0:T(8,128)(2,1)S(1)}, bf16[192,768]{1,0:T(8,128)(2,1)S(1)}, u32[]{:S(2)}, u32[]{:S(2)}) collective-permute-start(bf16[192,768]{1,0:T(8,128)(2,1)S(1)} %collective-permute-done.7.refs_0_), channel_id=1, source_target_pairs={{0,1},{1,2},{2,3},{3,4},{4,5},{5,6},{6,7},{7,0},{8,9},{9,10},{10,1... | collective-permute-start | bytes 884744 | tf_op jit(solution)/shard_map/ppermute | solution.py:18
  55.3 10.4 %collective-permute-start.13 = (bf16[192,768]{1,0:T(8,128)(2,1)S(1)}, bf16[192,768]{1,0:T(8,128)(2,1)S(1)}, u32[]{:S(2)}, u32[]{:S(2)}) collective-permute-start(bf16[192,768]{1,0:T(8,128)(2,1)S(1)} %collective-permute-done.9.refs_2_), channel_id=1, source_target_pairs={{0,1},{1,2},{2,3},{3,4},{4,5},{5,6},{6,7},{7,0},{8,9},{9,10},{10,1... | collective-permute-start | bytes 884744 | tf_op jit(solution)/shard_map/ppermute | solution.py:18
  61.6 6.7 %collective-permute-start.14 = (bf16[192,768]{1,0:T(8,128)(2,1)S(1)}, bf16[192,768]{1,0:T(8,128)(2,1)S(1)}, u32[]{:S(2)}, u32[]{:S(2)}) collective-permute-start(bf16[192,768]{1,0:T(8,128)(2,1)S(1)} %collective-permute-done.12.refs_5_), channel_id=1, source_target_pairs={{0,7},{1,0},{2,1},{3,2},{4,3},{5,4},{6,5},{7,6},{8,15},{9,8},{10,9... | collective-permute-start | bytes 884744 | tf_op jit(solution)/shard_map/ppermute | solution.py:18
  61.6 1.0 %copy-start.2 = (bf16[768,192]{0,1:T(8,128)(2,1)S(1)}, bf16[768,192]{0,1:T(8,128)(2,1)}, u32[]{:S(2)}) copy-start(bf16[768,192]{0,1:T(8,128)(2,1)} %param.6) | copy-start | bytes 884740
  62.6 0.7 copy-start.3
  63.3 0.7 copy-start.4
  65.6 5.9 %copy-start.5 = (s32[8]{0:T(128)S(1)}, s32[8]{0:T(128)}, u32[]{:S(2)}) copy-start(s32[8]{0:T(128)} %pair_ref.5) | copy-start | bytes 100
  65.7 5.8 %copy-start.6 = (s32[16]{0:T(128)S(1)}, s32[16]{0:T(128)}, u32[]{:S(2)}) copy-start(s32[16]{0:T(128)} %ab_ref.1) | copy-start | bytes 196
  70.1 1.4 %copy-start.1 = (bf16[768,1536]{1,0:T(8,128)(2,1)}, bf16[768,1536]{1,0:T(8,128)(2,1)S(1)}, u32[]{:S(2)}) copy-start(bf16[768,1536]{1,0:T(8,128)(2,1)S(1)} %arrange_amplitudes.3.late_ref) | copy-start | bytes 7077892
Sparse Core Ops, SparseCore 0:
  9.2 62.1 all-gather.2

commit v4 on v3

--- a/solution.py
+++ b/solution.py
@@ -88,7 +88,7 @@
         out_shape=jax.ShapeDtypeStruct(shape, chunks[0].dtype),
         in_specs=[smem, smem] + [vmem] * len(chunks),
         out_specs=vmem,
-        compiler_params=pltpu.CompilerParams(vmem_limit_bytes=24 << 20),
+        compiler_params=pltpu.CompilerParams(vmem_limit_bytes=28 << 20),
         cost_estimate=pl.CostEstimate(flops=10**8, bytes_accessed=10**7, transcendentals=0),
         name="arrange_amplitudes",
     )(pair_class, cd_class, *chunks)
@@ -151,7 +151,7 @@
 def finished(early, late, panel, prior, pair_class, ab_class):
     high, deep = early.shape
     width = panel.shape[2]
-    block = 256
+    block = 512
     steps = width // block
     smem, vmem = (pl.BlockSpec(memory_space=space) for space in (pltpu.SMEM, pltpu.VMEM))
     hbm = pl.BlockSpec(memory_space=pltpu.HBM)
@@ -169,7 +169,7 @@
             pltpu.SemaphoreType.DMA,
             pltpu.SemaphoreType.DMA((3, steps)),
         ],
-        compiler_params=pltpu.CompilerParams(vmem_limit_bytes=24 << 20),
+        compiler_params=pltpu.CompilerParams(vmem_limit_bytes=28 << 20),
         cost_estimate=pl.CostEstimate(flops=4 * high * deep * width, bytes_accessed=4 * deep * width, transcendentals=0),
         name="product",
     )(pair_class, ab_class, keep(early, pltpu.VMEM), keep(late, pltpu.HBM), keep(panel, pltpu.HBM), keep(prior, pltpu.HBM))

time: 92.7 us -> 92.6 us (level)
  no operation moved by 1% of the time
where the time goes in v4:
time: 92.6 us; the launch traced here: 90.9 us
  starting transfers between devices  28.4 us (31%)
  waiting for transfers between devices  27.1 us (29%)
  Pallas kernels  16 us (17%)
  between operations  13.5 us (15%)
  local copies, waits for them, and re-layouts  4.65 us (5%)
  matrix products  1.17 us (1%)
    ppermute x15, starting transfers between devices, shift(): lax.ppermute(value, axis, [(i, (i + steps) % count) for i in range(count)])  28.4 us
    ppermute x15, waiting for transfers between devices, shift(): lax.ppermute(value, axis, [(i, (i + steps) % count) for i in range(count)])  27.1 us
    pallas_call x1, Pallas kernels, finished(): pl.pallas_call(functools.partial(product_kernel, block), out_shape=jax.Sh...  12.5 us
    unnamed x14, local copies, waits for them, and re-layouts  4.47 us
    pallas_call x2, Pallas kernels, arranged(): pl.pallas_call(functools.partial(arrange_kernel, [place for _, *place in...  3.45 us
  transfers between devices with their start and end apart: 16, of which 9 were waited for; matrix products, arithmetic and copies ran while one was open for 0% of the time, Pallas kernels for 4%

profile of v4, /device:TPU:12, one launch (start us, length us, event | category | flops | bytes accessed | tf_op | source)
XLA Modules:
  0.0 90.9 jit_solution(2750687607424024164)
XLA Ops:
  6.5 0.0 copy-start
  6.5 0.0 all-gather.3.cloned.1.call-start
  6.5 0.1 stack.67
  6.6 0.1 broadcast_add_fusion
  6.7 0.1 add.166
  6.8 0.8 copy-done
  7.6 1.2 %convolution_convert_fusion = bf16[192,1536]{1,0:T(8,128)(2,1)} fusion(bf16[192,1536]{1,0:T(8,128)(2,1)S(1)} %bitcast.22, s32[192]{0:T(256)S(1)} %add.166), kind=kOutput, calls=%fused_computation | convolution fusion | flops 113577984 | bytes 1180416 | tf_op jit(solution)/shard_map/dot_general | solution.py:46
  8.8 0.0 all-gather.3.cloned.1.call-update
  8.8 2.4 %collective-permute-start = (bf16[192,768]{1,0:T(8,128)(2,1)}, bf16[192,768]{1,0:T(8,128)(2,1)S(1)}, u32[]{:S(2)}, u32[]{:S(2)}) collective-permute-start(bf16[192,768]{1,0:T(8,128)(2,1)} %bitcast.23), channel_id=1, source_target_pairs={{0,8},{8,0},{1,9},{9,1},{2,10},{10,2},{3,11},{11,3},{4,12},{12,4},... | collective-permute-start | bytes 884744 | tf_op jit(solution)/shard_map/ppermute | solution.py:18
  11.2 5.9 %collective-permute-start.2 = (bf16[192,768]{1,0:T(8,128)(2,1)}, bf16[192,768]{1,0:T(8,128)(2,1)S(1)}, u32[]{:S(2)}, u32[]{:S(2)}) collective-permute-start(bf16[192,768]{1,0:T(8,128)(2,1)} %bitcast.24), channel_id=1, source_target_pairs={{0,7},{1,0},{2,1},{3,2},{4,3},{5,4},{6,5},{7,6},{8,15},{9,8},{10,9... | collective-permute-start | bytes 884744 | tf_op jit(solution)/shard_map/ppermute | solution.py:18
  17.0 0.0 collective-permute-start.1
  17.0 2.3 %collective-permute-done.refs_1_ = bf16[192,768]{1,0:T(8,128)(2,1)S(1)} collective-permute-done((bf16[192,768]{1,0:T(8,128)(2,1)}, bf16[192,768]{1,0:T(8,128)(2,1)S(1)}, u32[]{:S(2)}, u32[]{:S(2)}) %collective-permute-start) | collective-permute-done | bytes 294944 | tf_op jit(solution)/shard_map/ppermute | solution.py:18
  19.4 5.9 %collective-permute-start.4 = (bf16[192,768]{1,0:T(8,128)(2,1)S(1)}, bf16[192,768]{1,0:T(8,128)(2,1)S(1)}, u32[]{:S(2)}, u32[]{:S(2)}) collective-permute-start(bf16[192,768]{1,0:T(8,128)(2,1)S(1)} %collective-permute-done.refs_1_), channel_id=1, source_target_pairs={{0,7},{1,0},{2,1},{3,2},{4,3},{5,4},{6,5},{7,6},{8,15},{9,8},{10,9... | collective-permute-start | bytes 884744 | tf_op jit(solution)/shard_map/ppermute | solution.py:18
  25.2 0.0 collective-permute-start.3
  25.2 0.0 collective-permute-done.2.refs_3_
  25.2 3.2 %collective-permute-start.6 = (bf16[192,768]{1,0:T(8,128)(2,1)S(1)}, bf16[192,768]{1,0:T(8,128)(2,1)S(1)}, u32[]{:S(2)}, u32[]{:S(2)}) collective-permute-start(bf16[192,768]{1,0:T(8,128)(2,1)S(1)} %collective-permute-done.2.refs_3_), channel_id=1, source_target_pairs={{0,7},{1,0},{2,1},{3,2},{4,3},{5,4},{6,5},{7,6},{8,15},{9,8},{10,9... | collective-permute-start | bytes 884744 | tf_op jit(solution)/shard_map/ppermute | solution.py:18
  28.4 0.0 collective-permute-done.1.refs_2_
  28.4 0.0 collective-permute-start.5
  28.5 4.2 %collective-permute-done.4.refs_5_ = bf16[192,768]{1,0:T(8,128)(2,1)S(1)} collective-permute-done((bf16[192,768]{1,0:T(8,128)(2,1)S(1)}, bf16[192,768]{1,0:T(8,128)(2,1)S(1)}, u32[]{:S(2)}, u32[]{:S(2)}) %collective-permute-start.4) | collective-permute-done | bytes 294944 | tf_op jit(solution)/shard_map/ppermute | solution.py:18
  32.7 3.7 %collective-permute-start.8 = (bf16[192,768]{1,0:T(8,128)(2,1)S(1)}, bf16[192,768]{1,0:T(8,128)(2,1)S(1)}, u32[]{:S(2)}, u32[]{:S(2)}) collective-permute-start(bf16[192,768]{1,0:T(8,128)(2,1)S(1)} %collective-permute-done.4.refs_5_), channel_id=1, source_target_pairs={{0,7},{1,0},{2,1},{3,2},{4,3},{5,4},{6,5},{7,6},{8,15},{9,8},{10,9... | collective-permute-start | bytes 884744 | tf_op jit(solution)/shard_map/ppermute | solution.py:18
  36.4 0.0 collective-permute-done.3.refs_4_
  36.4 0.0 collective-permute-start.7
  36.4 2.6 %collective-permute-done.6.refs_7_ = bf16[192,768]{1,0:T(8,128)(2,1)S(1)} collective-permute-done((bf16[192,768]{1,0:T(8,128)(2,1)S(1)}, bf16[192,768]{1,0:T(8,128)(2,1)S(1)}, u32[]{:S(2)}, u32[]{:S(2)}) %collective-permute-start.6) | collective-permute-done | bytes 294944 | tf_op jit(solution)/shard_map/ppermute | solution.py:18
  39.0 3.7 %collective-permute-start.10 = (bf16[192,768]{1,0:T(8,128)(2,1)S(1)}, bf16[192,768]{1,0:T(8,128)(2,1)S(1)}, u32[]{:S(2)}, u32[]{:S(2)}) collective-permute-start(bf16[192,768]{1,0:T(8,128)(2,1)S(1)} %collective-permute-done.6.refs_7_), channel_id=1, source_target_pairs={{0,7},{1,0},{2,1},{3,2},{4,3},{5,4},{6,5},{7,6},{8,15},{9,8},{10,9... | collective-permute-start | bytes 884744 | tf_op jit(solution)/shard_map/ppermute | solution.py:18
  42.7 0.0 collective-permute-done.5.refs_6_
  42.7 0.0 collective-permute-start.9
  42.7 2.6 %collective-permute-done.8.refs_1_ = bf16[192,768]{1,0:T(8,128)(2,1)S(1)} collective-permute-done((bf16[192,768]{1,0:T(8,128)(2,1)S(1)}, bf16[192,768]{1,0:T(8,128)(2,1)S(1)}, u32[]{:S(2)}, u32[]{:S(2)}) %collective-permute-start.8) | collective-permute-done | bytes 294944 | tf_op jit(solution)/shard_map/ppermute | solution.py:18
  45.3 3.7 %collective-permute-start.12 = (bf16[192,768]{1,0:T(8,128)(2,1)S(1)}, bf16[192,768]{1,0:T(8,128)(2,1)S(1)}, u32[]{:S(2)}, u32[]{:S(2)}) collective-permute-start(bf16[192,768]{1,0:T(8,128)(2,1)S(1)} %collective-permute-done.8.refs_1_), channel_id=1, source_target_pairs={{0,7},{1,0},{2,1},{3,2},{4,3},{5,4},{6,5},{7,6},{8,15},{9,8},{10,9... | collective-permute-start | bytes 884744 | tf_op jit(solution)/shard_map/ppermute | solution.py:18
  49.0 0.0 collective-permute-done.7.refs_0_
  49.0 0.0 collective-permute-start.11
  49.0 2.6 %collective-permute-done.10.refs_3_ = bf16[192,768]{1,0:T(8,128)(2,1)S(1)} collective-permute-done((bf16[192,768]{1,0:T(8,128)(2,1)S(1)}, bf16[192,768]{1,0:T(8,128)(2,1)S(1)}, u32[]{:S(2)}, u32[]{:S(2)}) %collective-permute-start.10) | collective-permute-done | bytes 294944 | tf_op jit(solution)/shard_map/ppermute | solution.py:18
  51.6 3.7 %collective-permute-done.9.refs_2_ = bf16[192,768]{1,0:T(8,128)(2,1)S(1)} collective-permute-done((bf16[192,768]{1,0:T(8,128)(2,1)S(1)}, bf16[192,768]{1,0:T(8,128)(2,1)S(1)}, u32[]{:S(2)}, u32[]{:S(2)}) %collective-permute-start.9) | collective-permute-done | bytes 294944 | tf_op jit(solution)/shard_map/ppermute | solution.py:18
  55.3 0.0 collective-permute-start.13
  55.3 0.6 collective-permute-done.12.refs_5_
  55.9 5.8 %collective-permute-done.11.refs_4_ = bf16[192,768]{1,0:T(8,128)(2,1)S(1)} collective-permute-done((bf16[192,768]{1,0:T(8,128)(2,1)S(1)}, bf16[192,768]{1,0:T(8,128)(2,1)S(1)}, u32[]{:S(2)}, u32[]{:S(2)}) %collective-permute-start.11) | collective-permute-done | bytes 294944 | tf_op jit(solution)/shard_map/ppermute | solution.py:18
  61.6 0.0 collective-permute-start.14
  61.6 1.0 %copy-done.2 = bf16[768,192]{0,1:T(8,128)(2,1)S(1)} copy-done((bf16[768,192]{0,1:T(8,128)(2,1)S(1)}, bf16[768,192]{0,1:T(8,128)(2,1)}, u32[]{:S(2)}) %copy-start.2) | copy-done | bytes 294936
  62.6 0.7 copy-done.3
  63.3 0.7 copy-done.4
  63.9 1.7 %arrange_amplitudes.2.early_ref = bf16[768,1536]{1,0:T(8,128)(2,1)S(1)} custom-call(s32[8]{0:T(128)S(1)} %copy-done.4, s32[32]{0:T(128)S(1)} %copy-done.3, bf16[192,768]{1,0:T(8,128)(2,1)S(1)} %bitcast.26, bf16[192,768]{1,0:T(8,128)(2,1)S(1)} %collective-permute-done.refs_1_, bf16[192,768]{1,0:T(8,128)(2,1)S(1)} %collective-permute-done.1.refs_2_, ...), custom_call_target="tpu_custom_call" | custom-call | flops 100000000 | bytes 10000000 | tf_op jit(solution)/shard_map/arrange_amplitudes/pallas_call | solution.py:86
  65.6 0.0 copy-start.5
  65.7 0.0 copy-start.6
  65.7 0.0 collective-permute-done.13.refs_6_
  65.7 2.7 %collective-permute-done.14.refs_7_ = bf16[192,768]{1,0:T(8,128)(2,1)S(1)} collective-permute-done((bf16[192,768]{1,0:T(8,128)(2,1)S(1)}, bf16[192,768]{1,0:T(8,128)(2,1)S(1)}, u32[]{:S(2)}, u32[]{:S(2)}) %collective-permute-start.14) | collective-permute-done | bytes 294944 | tf_op jit(solution)/shard_map/ppermute | solution.py:18
  68.4 1.7 %arrange_amplitudes.3.late_ref = bf16[768,1536]{1,0:T(8,128)(2,1)S(1)} custom-call(s32[8]{0:T(128)S(1)} %copy-done.4, s32[32]{0:T(128)S(1)} %copy-done.3, bf16[192,768]{1,0:T(8,128)(2,1)S(1)} %collective-permute-done.7.refs_0_, bf16[192,768]{1,0:T(8,128)(2,1)S(1)} %collective-permute-done.8.refs_1_, bf16[192,768]{1,0:T(8,128)(2,1)S(1)} %collective-permute-done.9.refs_2_, ...), custom_call_target="tpu_custom_call" | custom-call | flops 100000000 | bytes 10000000 | tf_op jit(solution)/shard_map/arrange_amplitudes/pallas_call | solution.py:86
  70.1 0.0 copy-start.1
  70.1 1.4 %copy-done.1 = bf16[768,1536]{1,0:T(8,128)(2,1)} copy-done((bf16[768,1536]{1,0:T(8,128)(2,1)}, bf16[768,1536]{1,0:T(8,128)(2,1)S(1)}, u32[]{:S(2)}) %copy-start.1) | copy-done | bytes 2359320
  71.5 12.5 %product.1 = bf16[768,1536]{1,0:T(8,128)(2,1)} custom-call(s32[8]{0:T(128)S(1)} %copy-done.5, s32[16]{0:T(128)S(1)} %copy-done.6, bf16[768,1536]{1,0:T(8,128)(2,1)S(1)} %arrange_amplitudes.2.early_ref, bf16[768,1536]{1,0:T(8,128)(2,1)} %copy-done.1, bf16[16,192,1536]{2,1,0:T(8,128)(2,1)} %bitcast.27, bf16[768,1536]{1,0:T(8,128)(2,1)} %prior_ref.1), custom_call_target="tpu_custom_call" | custom-call | flops 7247757312 | bytes 9437184 | tf_op jit(solution)/shard_map/product/pallas_call | solution.py:159
  (7 shorter events, 0.0 us)
Async XLA Ops:
  6.5 1.1 %copy-start = (bf16[16,12,1536]{2,0,1:T(8,128)(2,1)S(1)}, bf16[16,12,1536]{2,0,1:T(8,128)(2,1)}, u32[]{:S(2)}) copy-start(bf16[16,12,1536]{2,0,1:T(8,128)(2,1)} %param.7) | copy-start | bytes 1769476
  6.5 65.0 %all-gather.3.cloned.1.call-start = ((), (), s32[]{:S(2)}) async-start(), calls=%async_computation | async-start | bytes 10027008 | tf_op jit(solution)/shard_map/all_gather | solution.py:181
  8.8 10.6 %collective-permute-start = (bf16[192,768]{1,0:T(8,128)(2,1)}, bf16[192,768]{1,0:T(8,128)(2,1)S(1)}, u32[]{:S(2)}, u32[]{:S(2)}) collective-permute-start(bf16[192,768]{1,0:T(8,128)(2,1)} %bitcast.23), channel_id=1, source_target_pairs={{0,8},{8,0},{1,9},{9,1},{2,10},{10,2},{3,11},{11,3},{4,12},{12,4},... | collective-permute-start | bytes 884744 | tf_op jit(solution)/shard_map/ppermute | solution.py:18
  11.2 14.0 %collective-permute-start.2 = (bf16[192,768]{1,0:T(8,128)(2,1)}, bf16[192,768]{1,0:T(8,128)(2,1)S(1)}, u32[]{:S(2)}, u32[]{:S(2)}) collective-permute-start(bf16[192,768]{1,0:T(8,128)(2,1)} %bitcast.24), channel_id=1, source_target_pairs={{0,7},{1,0},{2,1},{3,2},{4,3},{5,4},{6,5},{7,6},{8,15},{9,8},{10,9... | collective-permute-start | bytes 884744 | tf_op jit(solution)/shard_map/ppermute | solution.py:18
  17.0 11.4 %collective-permute-start.1 = (bf16[192,768]{1,0:T(8,128)(2,1)}, bf16[192,768]{1,0:T(8,128)(2,1)S(1)}, u32[]{:S(2)}, u32[]{:S(2)}) collective-permute-start(bf16[192,768]{1,0:T(8,128)(2,1)} %bitcast.25), channel_id=1, source_target_pairs={{0,1},{1,2},{2,3},{3,4},{4,5},{5,6},{6,7},{7,0},{8,9},{9,10},{10,1... | collective-permute-start | bytes 884744 | tf_op jit(solution)/shard_map/ppermute | solution.py:18
  19.4 13.3 %collective-permute-start.4 = (bf16[192,768]{1,0:T(8,128)(2,1)S(1)}, bf16[192,768]{1,0:T(8,128)(2,1)S(1)}, u32[]{:S(2)}, u32[]{:S(2)}) collective-permute-start(bf16[192,768]{1,0:T(8,128)(2,1)S(1)} %collective-permute-done.refs_1_), channel_id=1, source_target_pairs={{0,7},{1,0},{2,1},{3,2},{4,3},{5,4},{6,5},{7,6},{8,15},{9,8},{10,9... | collective-permute-start | bytes 884744 | tf_op jit(solution)/shard_map/ppermute | solution.py:18
  25.2 11.2 %collective-permute-start.3 = (bf16[192,768]{1,0:T(8,128)(2,1)S(1)}, bf16[192,768]{1,0:T(8,128)(2,1)S(1)}, u32[]{:S(2)}, u32[]{:S(2)}) collective-permute-start(bf16[192,768]{1,0:T(8,128)(2,1)S(1)} %collective-permute-done.refs_1_), channel_id=1, source_target_pairs={{0,1},{1,2},{2,3},{3,4},{4,5},{5,6},{6,7},{7,0},{8,9},{9,10},{10,1... | collective-permute-start | bytes 884744 | tf_op jit(solution)/shard_map/ppermute | solution.py:18
  25.2 13.8 %collective-permute-start.6 = (bf16[192,768]{1,0:T(8,128)(2,1)S(1)}, bf16[192,768]{1,0:T(8,128)(2,1)S(1)}, u32[]{:S(2)}, u32[]{:S(2)}) collective-permute-start(bf16[192,768]{1,0:T(8,128)(2,1)S(1)} %collective-permute-done.2.refs_3_), channel_id=1, source_target_pairs={{0,7},{1,0},{2,1},{3,2},{4,3},{5,4},{6,5},{7,6},{8,15},{9,8},{10,9... | collective-permute-start | bytes 884744 | tf_op jit(solution)/shard_map/ppermute | solution.py:18
  28.4 14.2 %collective-permute-start.5 = (bf16[192,768]{1,0:T(8,128)(2,1)S(1)}, bf16[192,768]{1,0:T(8,128)(2,1)S(1)}, u32[]{:S(2)}, u32[]{:S(2)}) collective-permute-start(bf16[192,768]{1,0:T(8,128)(2,1)S(1)} %collective-permute-done.1.refs_2_), channel_id=1, source_target_pairs={{0,1},{1,2},{2,3},{3,4},{4,5},{5,6},{6,7},{7,0},{8,9},{9,10},{10,1... | collective-permute-start | bytes 884744 | tf_op jit(solution)/shard_map/ppermute | solution.py:18
  32.7 12.6 %collective-permute-start.8 = (bf16[192,768]{1,0:T(8,128)(2,1)S(1)}, bf16[192,768]{1,0:T(8,128)(2,1)S(1)}, u32[]{:S(2)}, u32[]{:S(2)}) collective-permute-start(bf16[192,768]{1,0:T(8,128)(2,1)S(1)} %collective-permute-done.4.refs_5_), channel_id=1, source_target_pairs={{0,7},{1,0},{2,1},{3,2},{4,3},{5,4},{6,5},{7,6},{8,15},{9,8},{10,9... | collective-permute-start | bytes 884744 | tf_op jit(solution)/shard_map/ppermute | solution.py:18
  36.4 12.6 %collective-permute-start.7 = (bf16[192,768]{1,0:T(8,128)(2,1)S(1)}, bf16[192,768]{1,0:T(8,128)(2,1)S(1)}, u32[]{:S(2)}, u32[]{:S(2)}) collective-permute-start(bf16[192,768]{1,0:T(8,128)(2,1)S(1)} %collective-permute-done.3.refs_4_), channel_id=1, source_target_pairs={{0,1},{1,2},{2,3},{3,4},{4,5},{5,6},{6,7},{7,0},{8,9},{9,10},{10,1... | collective-permute-start | bytes 884744 | tf_op jit(solution)/shard_map/ppermute | solution.py:18
  39.0 12.6 %collective-permute-start.10 = (bf16[192,768]{1,0:T(8,128)(2,1)S(1)}, bf16[192,768]{1,0:T(8,128)(2,1)S(1)}, u32[]{:S(2)}, u32[]{:S(2)}) collective-permute-start(bf16[192,768]{1,0:T(8,128)(2,1)S(1)} %collective-permute-done.6.refs_7_), channel_id=1, source_target_pairs={{0,7},{1,0},{2,1},{3,2},{4,3},{5,4},{6,5},{7,6},{8,15},{9,8},{10,9... | collective-permute-start | bytes 884744 | tf_op jit(solution)/shard_map/ppermute | solution.py:18
  42.7 12.6 %collective-permute-start.9 = (bf16[192,768]{1,0:T(8,128)(2,1)S(1)}, bf16[192,768]{1,0:T(8,128)(2,1)S(1)}, u32[]{:S(2)}, u32[]{:S(2)}) collective-permute-start(bf16[192,768]{1,0:T(8,128)(2,1)S(1)} %collective-permute-done.5.refs_6_), channel_id=1, source_target_pairs={{0,1},{1,2},{2,3},{3,4},{4,5},{5,6},{6,7},{7,0},{8,9},{9,10},{10,1... | collective-permute-start | bytes 884744 | tf_op jit(solution)/shard_map/ppermute | solution.py:18
  45.3 10.6 %collective-permute-start.12 = (bf16[192,768]{1,0:T(8,128)(2,1)S(1)}, bf16[192,768]{1,0:T(8,128)(2,1)S(1)}, u32[]{:S(2)}, u32[]{:S(2)}) collective-permute-start(bf16[192,768]{1,0:T(8,128)(2,1)S(1)} %collective-permute-done.8.refs_1_), channel_id=1, source_target_pairs={{0,7},{1,0},{2,1},{3,2},{4,3},{5,4},{6,5},{7,6},{8,15},{9,8},{10,9... | collective-permute-start | bytes 884744 | tf_op jit(solution)/shard_map/ppermute | solution.py:18
  49.0 12.6 %collective-permute-start.11 = (bf16[192,768]{1,0:T(8,128)(2,1)S(1)}, bf16[192,768]{1,0:T(8,128)(2,1)S(1)}, u32[]{:S(2)}, u32[]{:S(2)}) collective-permute-start(bf16[192,768]{1,0:T(8,128)(2,1)S(1)} %collective-permute-done.7.refs_0_), channel_id=1, source_target_pairs={{0,1},{1,2},{2,3},{3,4},{4,5},{5,6},{6,7},{7,0},{8,9},{9,10},{10,1... | collective-permute-start | bytes 884744 | tf_op jit(solution)/shard_map/ppermute | solution.py:18
  55.3 10.4 %collective-permute-start.13 = (bf16[192,768]{1,0:T(8,128)(2,1)S(1)}, bf16[192,768]{1,0:T(8,128)(2,1)S(1)}, u32[]{:S(2)}, u32[]{:S(2)}) collective-permute-start(bf16[192,768]{1,0:T(8,128)(2,1)S(1)} %collective-permute-done.9.refs_2_), channel_id=1, source_target_pairs={{0,1},{1,2},{2,3},{3,4},{4,5},{5,6},{6,7},{7,0},{8,9},{9,10},{10,1... | collective-permute-start | bytes 884744 | tf_op jit(solution)/shard_map/ppermute | solution.py:18
  61.6 6.7 %collective-permute-start.14 = (bf16[192,768]{1,0:T(8,128)(2,1)S(1)}, bf16[192,768]{1,0:T(8,128)(2,1)S(1)}, u32[]{:S(2)}, u32[]{:S(2)}) collective-permute-start(bf16[192,768]{1,0:T(8,128)(2,1)S(1)} %collective-permute-done.12.refs_5_), channel_id=1, source_target_pairs={{0,7},{1,0},{2,1},{3,2},{4,3},{5,4},{6,5},{7,6},{8,15},{9,8},{10,9... | collective-permute-start | bytes 884744 | tf_op jit(solution)/shard_map/ppermute | solution.py:18
  61.6 1.0 %copy-start.2 = (bf16[768,192]{0,1:T(8,128)(2,1)S(1)}, bf16[768,192]{0,1:T(8,128)(2,1)}, u32[]{:S(2)}) copy-start(bf16[768,192]{0,1:T(8,128)(2,1)} %param.6) | copy-start | bytes 884740
  62.6 0.7 copy-start.3
  63.3 0.7 copy-start.4
  65.6 5.9 %copy-start.5 = (s32[8]{0:T(128)S(1)}, s32[8]{0:T(128)}, u32[]{:S(2)}) copy-start(s32[8]{0:T(128)} %pair_ref.5) | copy-start | bytes 100
  65.7 5.8 %copy-start.6 = (s32[16]{0:T(128)S(1)}, s32[16]{0:T(128)}, u32[]{:S(2)}) copy-start(s32[16]{0:T(128)} %ab_ref.1) | copy-start | bytes 196
  70.1 1.4 %copy-start.1 = (bf16[768,1536]{1,0:T(8,128)(2,1)}, bf16[768,1536]{1,0:T(8,128)(2,1)S(1)}, u32[]{:S(2)}) copy-start(bf16[768,1536]{1,0:T(8,128)(2,1)S(1)} %arrange_amplitudes.3.late_ref) | copy-start | bytes 7077892
Sparse Core Ops, SparseCore 0:
  9.2 62.1 all-gather.2
